TPU v7x, 128 devices: a whole 4x4x4 slice. The times are simulated.
128 devices in a mesh: half: 2 (over y_hi), row: 8 (over y_lo, z), col: 8 (over x, core).
Axes of the slice: x: 4, y: 4 (y_hi: 2, y_lo: 2; y = y_hi * 2 + y_lo), z: 4, core: 2. Of those that a mesh axis runs over, the one named last changes fastest.
Arguments:
- child_block: bfloat16 [2, 8, 8, 256, 8, 8, 256], P('half', None, 'row', None, None, 'col'), may hold values from -6 to 6
- child_row: bfloat16 [2, 256, 8, 8, 256], P('half', 'row', None, 'col'), may hold values from -6 to 6
- child_col: bfloat16 [2, 256, 8, 8, 256], P('half', 'col', None, 'row'), may hold values from -0.375 to 0.375
- child_pivot_inv: bfloat16 [2, 256, 256], P('half'), may hold values from -0.375 to 0.375
- child_map: int32 [2, 64], replicated, may hold values from 0 to 126, as said below
- parent_row: bfloat16 [256, 8, 16, 256], P('row', None, ('half', 'col')), may hold values from -6 to 6
- parent_col: bfloat16 [256, 16, 8, 256], P(('half', 'col'), None, 'row'), may hold values from -0.375 to 0.375
- parent_pivot_inv: bfloat16 [256, 256], replicated, may hold values from -0.375 to 0.375
- parent_diag: float32 [16, 8, 256], P(None, 'row'), may hold values from 1 to 3
Outputs:
- schur: bfloat16 [16, 8, 256, 8, 16, 256], P(None, 'row', None, None, ('half', 'col'))
Inputs may be any that keep to these rules, and one draw needn't show every extreme that they name: child_map[h, 8 * k + r] = 2 * 8 * k + r + p_h[k] for k and r from 0 to 7, where p_0 and p_1 are permutations of 0 to 7.
All inputs are finite; a program needn't handle non-finite values.
Results may differ from a plain program's by a relative error of at most 0.0041.
The roundings to bfloat16 on the way count: a program that leaves them out, or rounds other values in their place, can miss the bound.
Values may be sent and summed in bfloat16 or wider, within the bound.
A program may use at most 384 MiB of HBM per device.

v0:
```python
import jax
import jax.numpy as jnp
from jax import lax
from jax.sharding import PartitionSpec as P


def inverse_maps(child_map, parent_tiles):
    targets = jnp.arange(parent_tiles, dtype=jnp.int32)
    matches = child_map[:, None, :] == targets[None, :, None]
    covered = jnp.any(matches, axis=2)
    positions = jnp.arange(child_map.shape[1], dtype=jnp.int32)
    sources = jnp.sum(jnp.where(matches, positions[None, None, :], 0), axis=2)
    return (covered, sources)


def pick_index(keys, wanted):
    positions = jnp.arange(keys.shape[0], dtype=jnp.int32)
    matched = keys[None, :] == wanted[:, None]
    return (jnp.sum(jnp.where(matched, positions[None, :], 0), axis=1), jnp.any(matched, axis=1))


def shards(
    child_block,
    child_row,
    child_col,
    child_pivot_inv,
    child_map,
    parent_row,
    parent_col,
    parent_pivot_inv,
    parent_diag,
):
    grid_size = lax.axis_size("row")
    tile_width = child_pivot_inv.shape[-1]
    my_half = lax.axis_index("half")
    my_row = lax.axis_index("row")
    my_col = lax.axis_index("col")
    local_width = grid_size * tile_width
    parent_height = 2 * grid_size * tile_width
    child_inv = child_pivot_inv[0]
    pieces = (
        lax.all_gather(child_row[0], "row", axis=0, tiled=True),
        lax.all_gather(parent_row, "row", axis=0, tiled=True),
    )
    piece_rows = pieces[0].shape[0]
    child_piece = pieces[0].reshape(piece_rows, local_width)
    parent_piece = pieces[1].reshape(piece_rows, local_width)
    child_sum = jnp.dot(child_inv, child_piece, preferred_element_type=jnp.float32)
    parent_sum = jnp.dot(parent_pivot_inv, parent_piece, preferred_element_type=jnp.float32)
    child_scaled = child_sum
    parent_scaled = parent_sum
    child_scaled = child_scaled.astype(jnp.bfloat16)
    parent_scaled = parent_scaled.astype(jnp.bfloat16)
    piece = lax.all_gather(child_col, "col", axis=1, tiled=True)
    piece_rows = piece.shape[1]
    flattened = piece.reshape(piece_rows, local_width)
    scaled_part = child_scaled
    child_update = lax.dot_general(
        flattened, scaled_part, (((0,), (0,)), ((), ())), preferred_element_type=jnp.float32
    )
    contribution = (
        child_block.reshape(local_width, local_width).astype(jnp.float32) - child_update
    ).astype(jnp.bfloat16)
    tile_grid = contribution.reshape(grid_size, tile_width, grid_size, tile_width)
    parent_rows = grid_size * jnp.arange(2 * grid_size, dtype=jnp.int32) + my_row
    column_slot = my_half * grid_size + my_col
    parent_columns = 2 * grid_size * jnp.arange(grid_size, dtype=jnp.int32) + column_slot
    diag_values = parent_diag.reshape(2 * grid_size, tile_width)
    on_diagonal = (parent_rows[:, None] == parent_columns[None, :]).astype(jnp.float32)
    identity = jnp.eye(tile_width, dtype=jnp.float32)
    diag_term = (
        diag_values[:, :, None, None] * on_diagonal[:, None, :, None] * identity[None, :, None, :]
    ).reshape(parent_height, local_width)
    piece = lax.all_gather(parent_col, ("half", "col"), axis=0, tiled=True)
    piece_rows = piece.shape[0]
    flattened = piece.reshape(piece_rows, parent_height)
    scaled_part = parent_scaled
    parent_front = diag_term - lax.dot_general(
        flattened, scaled_part, (((0,), (0,)), ((), ())), preferred_element_type=jnp.float32
    )
    covered, sources = inverse_maps(child_map, 2 * grid_size * grid_size)
    own_map = jnp.take(child_map, my_half, axis=0).reshape(grid_size, grid_size)
    row_targets = lax.dynamic_index_in_dim(own_map, my_row, 1, keepdims=False)
    col_targets = lax.dynamic_index_in_dim(own_map, my_col, 1, keepdims=False)
    slots_small = jnp.arange(grid_size, dtype=jnp.int32)
    row_pick, row_found = pick_index(row_targets % grid_size, slots_small)
    row_covered = covered[:, parent_rows]
    row_source = sources[:, parent_rows] % grid_size
    col_covered = covered[:, parent_columns]
    col_source = sources[:, parent_columns] % grid_size
    usable = row_covered[:, :, None] & col_covered[:, None, :]
    by_rows = jnp.take(tile_grid, row_pick, axis=0)
    column_slots = jnp.arange(2 * grid_size, dtype=jnp.int32)
    col_pick, col_live = pick_index(col_targets % (2 * grid_size), column_slots)
    packed = jnp.take(by_rows, col_pick, axis=2)
    packed = jnp.where(col_live[None, None, :, None], packed, jnp.zeros((), jnp.bfloat16))
    moved_rows = lax.all_to_all(packed, "row", split_axis=0, concat_axis=0, tiled=True)
    arrived = lax.all_to_all(moved_rows, ("half", "col"), split_axis=2, concat_axis=2, tiled=True)
    sibling_pieces = []
    for sibling in range(2):
        picked = jnp.take(arrived, row_source[sibling], axis=0)
        sibling_pieces.append(jnp.take(picked, sibling * grid_size + col_source[sibling], axis=2))
    front_blocks = parent_front.reshape(2 * grid_size, tile_width, grid_size, tile_width)
    for sibling in range(2):
        mask = usable[sibling][:, None, :, None]
        front_blocks = front_blocks + jnp.where(
            mask, sibling_pieces[sibling].astype(jnp.float32), 0.0
        )
    schur_front = front_blocks.astype(jnp.bfloat16)
    return schur_front.reshape(2 * grid_size, 1, tile_width, grid_size, 1, tile_width)


def solution(mesh):
    return jax.shard_map(
        shards,
        mesh=mesh,
        in_specs=(
            P("half", None, "row", None, None, "col", None),
            P("half", "row", None, "col", None),
            P("half", "col", None, "row", None),
            P("half", None, None),
            P(),
            P("row", None, ("half", "col"), None),
            P(("half", "col"), None, "row", None),
            P(),
            P(None, "row", None),
        ),
        out_specs=P(None, "row", None, None, ("half", "col"), None),
        check_vma=False,
    )
```

profile of v0, /device:TPU:15, one launch (start us, length us, event | category | flops | bytes accessed | tf_op | source)
XLA Modules:
  0.0 911.3 jit_solution(1902297807044894404)
XLA Ops:
  8.8 13.8 %copy.75 = f32[256,8,8,256]{3,1,2,0:T(8,128)} copy(bf16[256,8,8,256]{3,2,1,0:T(8,128)(2,1)} %bitcast.101) | data formatting | bytes 25165824
  22.6 18.1 %copy.67 = f32[2048,2048]{0,1:T(8,128)} copy(f32[2048,2048]{1,0:T(8,128)} %bitcast.94) | data formatting | bytes 33554432 | tf_op jit(solution)/shard_map/convert_element_type | solution.py:62
  45.6 27.4 %all-gather.10.cloned.1.call-done = bf16[1,256,8,1,256]{4,2,3,0,1:T(8,128)(2,1)} async-done(((bf16[1,32,8,1,256]{4,2,3,0,1:T(8,128)(2,1)}), bf16[1,256,8,1,256]{4,2,3,0,1:T(8,128)(2,1)}) %all-gather.10.cloned.1.call-update) | async-done | bytes 1048592 | tf_op jit(solution)/shard_map/all_gather | solution.py:54
  74.6 9.3 %fusion.1 = bf16[2048,2048]{0,1:T(8,128)(2,1)} fusion(f32[2048,2048]{0,1:T(8,128)} %copy.67, bf16[256,2048]{1,0:T(8,128)(2,1)S(1)} %bitcast.105, bf16[256,2048]{1,0:T(8,128)(2,1)S(1)} %bitcast.104, bf16[1,256,256]{2,1,0:T(8,128)(2,1)S(1)} %copy-done.2), kind=kOutput, calls=%fused_computation.22 | convolution fusion | flops 2424832000 | bytes 27394048 | tf_op jit(solution)/shard_map/dot_general | solution.py:58
  83.9 10.3 %copy.78 = bf16[256,8,8,256]{3,2,1,0:T(8,128)(2,1)} copy(bf16[256,8,8,256]{3,1,2,0:T(8,128)(2,1)} %bitcast.99) | data formatting | bytes 16777216
  94.1 12.6 %copy.58 = bf16[8,256,8,256]{3,1,2,0:T(8,128)(2,1)} copy(bf16[8,256,8,256]{1,0,3,2:T(8,128)(2,1)} %bitcast.100) | data formatting | bytes 16777216 | tf_op jit(solution)/shard_map/reshape | solution.py:64
  106.7 8.1 gather_fusion.2
  122.2 10.5 %gather_fusion.3 = bf16[16,8,256,256]{3,2,1,0:T(8,128)(2,1)} fusion(bf16[8,256,8,256]{3,1,2,0:T(8,128)(2,1)} %broadcast_select_fusion, s32[1024]{0:T(1024)S(1)} %pad_clamp_fusion.4), kind=kCustom, calls=%fused_computation.11 | custom fusion | bytes 33554496 | tf_op jit(solution)/shard_map/jit(_take)/gather | solution.py:95
  132.8 8.7 select_bitcast_fusion
  143.7 187.3 %all_to_all.10 = bf16[8,256,16,256]{3,1,2,0:T(8,128)(2,1)S(1)} all-to-all(bf16[8,256,16,256]{3,1,2,0:T(8,128)(2,1)S(1)} %copy.59), channel_id=1, replica_groups=mesh['half'=2,'row'=8,'col'=8] {'row'}, dimensions={0} | all-to-all | bytes 33554432 | tf_op jit(solution)/shard_map/all_to_all | solution.py:97
  337.6 8.8 all-to-all-start.1
  355.4 36.2 %copy.71 = f32[256,8,16,256]{3,1,2,0:T(8,128)} copy(f32[256,8,16,256]{3,2,1,0:T(8,128)S(1)} %bitcast.92) | data formatting | bytes 67108864
  395.1 57.6 %all-gather.6.cloned.1.call-done = bf16[256,8,1,256]{3,1,2,0:T(8,128)(2,1)} async-done(((bf16[32,8,1,256]{3,1,2,0:T(8,128)(2,1)}), bf16[256,8,1,256]{3,1,2,0:T(8,128)(2,1)}) %all-gather.6.cloned.1.call-update) | async-done | bytes 1048592 | tf_op jit(solution)/shard_map/all_gather | solution.py:43
  454.3 124.2 %all-gather.8.cloned.1.call-done = bf16[256,16,1,256]{3,1,2,0:T(8,128)(2,1)} async-done(((bf16[16,16,1,256]{3,1,2,0:T(8,128)(2,1)}), bf16[256,16,1,256]{3,1,2,0:T(8,128)(2,1)}) %all-gather.8.cloned.1.call-update) | async-done | bytes 2097168 | tf_op jit(solution)/shard_map/all_gather | solution.py:74
  581.0 21.5 %bitcast_subtract_fusion = f32[4096,2048]{0,1:T(8,128)} fusion(f32[4096,2048]{0,1:T(8,128)} %bitcast.90, bf16[256,4096]{1,0:T(8,128)(2,1)S(1)} %bitcast.102, bf16[256,256]{1,0:T(8,128)(2,1)S(1)} %copy-done, bf16[256,2048]{1,0:T(8,128)(2,1)S(1)} %bitcast.103), kind=kOutput, calls=%fused_computation.16 | convolution fusion | flops 4572315648 | bytes 70385664 | tf_op jit(solution)/shard_map/dot_general | solution.py:78
  602.5 30.2 %copy.74 = f32[256,8,16,256]{3,2,1,0:T(8,128)} copy(f32[256,8,16,256]{3,1,2,0:T(8,128)} %bitcast.91) | data formatting | bytes 67108864
  632.7 34.4 %copy.63 = f32[16,256,8,256]{3,1,0,2:T(8,128)} copy(f32[16,256,8,256]{1,0,3,2:T(8,128)} %bitcast.93) | data formatting | bytes 67108864 | tf_op jit(solution)/shard_map/reshape | solution.py:103
  667.2 12.0 %fusion.18 = (bf16[8,128,16,256]{3,1,0,2:T(8,128)(2,1)}, bf16[8,128,16,256]{3,1,0,2:T(8,128)(2,1)}) fusion(bf16[8,256,16,256]{3,1,0,2:T(8,128)(2,1)} %all-to-all-done.1), kind=kLoop, calls=%fused_computation.102 | loop fusion | bytes 33554432 | tf_op jit(solution)/shard_map/jit(_take)/gather | solution.py:101
  694.6 10.5 %gather_fusion.11 = bf16[16,128,16,256]{3,1,2,0:T(8,128)(2,1)} fusion(bf16[8,128,16,256]{3,1,2,0:T(8,128)(2,1)} %copy.70, s32[1024]{0:T(1024)S(1)} %pad_clamp_fusion.1), kind=kCustom, calls=%fused_computation.5.clone | custom fusion | bytes 33554496 | tf_op jit(solution)/shard_map/jit(_take)/gather | solution.py:101
  705.1 10.7 %gather_fusion.7 = bf16[16,128,16,256]{3,1,2,0:T(8,128)(2,1)} fusion(bf16[8,128,16,256]{3,1,2,0:T(8,128)(2,1)} %copy.70, s32[1024]{0:T(1024)S(1)} %pad_clamp_fusion.3), kind=kCustom, calls=%fused_computation.1.clone | custom fusion | bytes 33554496 | tf_op jit(solution)/shard_map/jit(_take)/gather | solution.py:101
  715.8 10.5 %gather_fusion.6 = bf16[16,128,16,256]{3,1,2,0:T(8,128)(2,1)} fusion(bf16[8,128,16,256]{3,1,2,0:T(8,128)(2,1)} %copy.69, s32[1024]{0:T(1024)S(1)} %pad_clamp_fusion.3), kind=kCustom, calls=%fused_computation.clone | custom fusion | bytes 33554496 | tf_op jit(solution)/shard_map/jit(_take)/gather | solution.py:101
  726.3 10.5 %gather_fusion.10 = bf16[16,128,16,256]{3,1,2,0:T(8,128)(2,1)} fusion(bf16[8,128,16,256]{3,1,2,0:T(8,128)(2,1)} %copy.69, s32[1024]{0:T(1024)S(1)} %pad_clamp_fusion.1), kind=kCustom, calls=%fused_computation.4.clone | custom fusion | bytes 33554496 | tf_op jit(solution)/shard_map/jit(_take)/gather | solution.py:101
  736.8 22.6 %maximum_select_fusion = bf16[16,256,16,256]{3,1,2,0:T(8,128)(2,1)} fusion(bf16[16,128,16,256]{3,1,2,0:T(8,128)(2,1)} %gather_fusion.7, bf16[16,128,16,256]{3,1,2,0:T(8,128)(2,1)} %gather_fusion.6, pred[16]{0:T(512)(128)(4,1)S(1)} %get-tuple-element.39), kind=kLoop, calls=%fused_computation.14 | loop fusion | flops 83886080 | bytes 67108880 | tf_op jit(solution)/shard_map/jit(_take)/select_n | solution.py:101
  759.4 23.3 %fusion.17 = (bf16[16,128,16,256]{3,1,2,0:T(8,128)(2,1)}, bf16[16,128,16,256]{3,1,2,0:T(8,128)(2,1)}) fusion(bf16[16,256,16,256]{3,1,2,0:T(8,128)(2,1)} %maximum_select_fusion), kind=kLoop, calls=%fused_computation.101 | loop fusion | bytes 67108864 | tf_op jit(solution)/shard_map/jit(_take)/gather | solution.py:102
  782.7 10.6 %gather_fusion.8 = bf16[8,16,128,256]{3,2,1,0:T(8,128)(2,1)} fusion(bf16[16,128,16,256]{3,1,2,0:T(8,128)(2,1)} %get-tuple-element.26, s32[1024]{0:T(1024)} %pad_clamp_fusion.2), kind=kCustom, calls=%fused_computation.2.clone | custom fusion | bytes 16777248 | tf_op jit(solution)/shard_map/jit(_take)/gather | solution.py:102
  793.3 10.6 %gather_fusion.9 = bf16[8,16,128,256]{3,2,1,0:T(8,128)(2,1)} fusion(bf16[16,128,16,256]{3,1,2,0:T(8,128)(2,1)} %get-tuple-element.27, s32[1024]{0:T(1024)} %pad_clamp_fusion.2), kind=kCustom, calls=%fused_computation.3.clone | custom fusion | bytes 16777248 | tf_op jit(solution)/shard_map/jit(_take)/gather | solution.py:102
  803.9 22.6 %maximum_select_fusion.1 = bf16[16,256,16,256]{3,1,2,0:T(8,128)(2,1)} fusion(bf16[16,128,16,256]{3,1,2,0:T(8,128)(2,1)} %gather_fusion.11, bf16[16,128,16,256]{3,1,2,0:T(8,128)(2,1)} %gather_fusion.10, pred[16]{0:T(512)(128)(4,1)S(1)} %copy-done.9), kind=kLoop, calls=%fused_computation.15 | loop fusion | flops 83886080 | bytes 67108880 | tf_op jit(solution)/shard_map/jit(_take)/select_n | solution.py:101
  826.6 23.3 %fusion.16 = (bf16[16,128,16,256]{3,1,2,0:T(8,128)(2,1)}, bf16[16,128,16,256]{3,1,2,0:T(8,128)(2,1)}) fusion(bf16[16,256,16,256]{3,1,2,0:T(8,128)(2,1)} %maximum_select_fusion.1), kind=kLoop, calls=%fused_computation.100 | loop fusion | bytes 67108864 | tf_op jit(solution)/shard_map/jit(_take)/gather | solution.py:102
  849.9 10.6 %gather_fusion.12 = bf16[8,16,128,256]{3,2,1,0:T(8,128)(2,1)} fusion(bf16[16,128,16,256]{3,1,2,0:T(8,128)(2,1)} %get-tuple-element.24, s32[1024]{0:T(1024)} %pad_clamp_fusion), kind=kCustom, calls=%fused_computation.6.clone | custom fusion | bytes 16777248 | tf_op jit(solution)/shard_map/jit(_take)/gather | solution.py:102
  860.5 10.7 %gather_fusion.13 = bf16[8,16,128,256]{3,2,1,0:T(8,128)(2,1)} fusion(bf16[16,128,16,256]{3,1,2,0:T(8,128)(2,1)} %get-tuple-element.25, s32[1024]{0:T(1024)} %pad_clamp_fusion), kind=kCustom, calls=%fused_computation.7.clone | custom fusion | bytes 16777248 | tf_op jit(solution)/shard_map/jit(_take)/gather | solution.py:102
  871.3 22.2 %fusion = bf16[16,1,256,8,1,256]{5,2,0,3,4,1:T(8,128)(2,1)S(1)} fusion(f32[16,256,8,256]{3,1,0,2:T(8,128)} %copy.63, bf16[16,128,8,256]{3,1,0,2:T(8,128)(2,1)} %bitcast.96, bf16[16,128,8,256]{3,1,0,2:T(8,128)(2,1)} %bitcast.95, bf16[16,128,8,256]{3,1,0,2:T(8,128)(2,1)} %bitcast.98, bf16[16,128,8,256]{3,1,0,2:T(8,128)(2,1)} %bitcast.97, ...), kind=kLoop, calls=%fused_computation.18 | loop fusion | flops 142606336 | bytes 83886352 | tf_op jit(solution)/shard_map/reshape | solution.py:110
  893.5 11.1 %copy.66 = bf16[16,1,256,8,1,256]{5,3,4,2,1,0:T(8,128)(2,1)} copy(bf16[16,1,256,8,1,256]{5,2,0,3,4,1:T(8,128)(2,1)S(1)} %fusion) | data formatting | bytes 33554432 | tf_op jit(solution)/shard_map/reshape | solution.py:110
  (87 shorter events, 56.7 us)
Async XLA Ops:
  6.5 574.5 %copy-start = (bf16[256,256]{1,0:T(8,128)(2,1)S(1)}, bf16[256,256]{1,0:T(8,128)(2,1)}, u32[]{:S(2)}) copy-start(bf16[256,256]{1,0:T(8,128)(2,1)} %param.20) | copy-start | bytes 393220
  6.5 37.6 %all-gather.12.cloned.1.call-start = ((), (), s32[]{:S(2)}) async-start(), calls=%async_computation.5 | async-start | bytes 1179648 | tf_op jit(solution)/shard_map/all_gather | solution.py:42
  7.3 65.8 %all-gather.10.cloned.1.call-start = ((), (), s32[]{:S(2)}) async-start(), calls=%async_computation.4 | async-start | bytes 1179648 | tf_op jit(solution)/shard_map/all_gather | solution.py:54
  22.6 51.9 %copy-start.2 = (bf16[1,256,256]{2,1,0:T(8,128)(2,1)S(1)}, bf16[1,256,256]{2,1,0:T(8,128)(2,1)}, u32[]{:S(2)}) copy-start(bf16[1,256,256]{2,1,0:T(8,128)(2,1)} %param.16) | copy-start | bytes 393220
  337.5 10.2 %copy-start.6 = (s32[2,64]{1,0:T(2,128)S(1)}, s32[2,64]{1,0:T(2,128)}, u32[]{:S(2)}) copy-start(s32[2,64]{1,0:T(2,128)} %param.17) | copy-start | bytes 1540
  337.5 13.1 %copy-start.3 = (f32[16,1,256]{2,1,0:T(1,128)S(1)}, f32[16,1,256]{2,1,0:T(1,128)}, u32[]{:S(2)}) copy-start(f32[16,1,256]{2,1,0:T(1,128)} %param.21) | copy-start | bytes 49156
  337.6 329.6 %all-to-all-start.1 = ((bf16[8,256,16,256]{3,1,0,2:T(8,128)(2,1)}), bf16[8,256,16,256]{3,1,0,2:T(8,128)(2,1)}, u32[]{:S(2)}, u32[]{:S(2)}) async-start(bf16[8,256,16,256]{3,1,0,2:T(8,128)(2,1)} %copy.60), calls=%async_computation.1 | async-start | bytes 33554432 | tf_op jit(solution)/shard_map/all_to_all | solution.py:98
  346.4 106.3 %all-gather.6.cloned.1.call-start = ((), (), s32[]{:S(2)}) async-start(), calls=%async_computation.2 | async-start | bytes 1179648 | tf_op jit(solution)/shard_map/all_gather | solution.py:43
  347.1 231.4 %all-gather.8.cloned.1.call-start = ((), (), s32[]{:S(2)}) async-start(), calls=%async_computation.3 | async-start | bytes 2228224 | tf_op jit(solution)/shard_map/all_gather | solution.py:74
  782.7 21.2 %copy-start.9 = (pred[16]{0:T(512)(128)(4,1)S(1)}, pred[16]{0:T(512)(128)(4,1)}, u32[]{:S(2)}) copy-start(pred[16]{0:T(512)(128)(4,1)} %get-tuple-element.38) | copy-start | bytes 52
  849.9 21.3 %copy-start.4 = (pred[16,8]{0,1:T(8,128)(4,1)S(1)}, pred[16,8]{0,1:T(8,128)(4,1)}, u32[]{:S(2)}) copy-start(pred[16,8]{0,1:T(8,128)(4,1)} %get-tuple-element.30) | copy-start | bytes 388
  849.9 21.3 %copy-start.5 = (pred[16,8]{0,1:T(8,128)(4,1)S(1)}, pred[16,8]{0,1:T(8,128)(4,1)}, u32[]{:S(2)}) copy-start(pred[16,8]{0,1:T(8,128)(4,1)} %get-tuple-element.31) | copy-start | bytes 388
  849.9 21.3 %copy-start.7 = (pred[8]{0:T(512)(128)(4,1)S(1)}, pred[8]{0:T(512)(128)(4,1)}, u32[]{:S(2)}) copy-start(pred[8]{0:T(512)(128)(4,1)} %get-tuple-element.36) | copy-start | bytes 28
  849.9 21.3 %copy-start.8 = (pred[8]{0:T(512)(128)(4,1)S(1)}, pred[8]{0:T(512)(128)(4,1)}, u32[]{:S(2)}) copy-start(pred[8]{0:T(512)(128)(4,1)} %get-tuple-element.37) | copy-start | bytes 28
  871.3 33.3 %copy-start.1 = (bf16[256,256]{1,0:T(8,128)(2,1)S(1)}, bf16[256,256]{1,0:T(8,128)(2,1)}, u32[]{:S(2)}) copy-start(bf16[256,256]{1,0:T(8,128)(2,1)} %param.20) | copy-start | bytes 393220
Sparse Core Ops, SparseCore 0:
  9.0 35.0 all-gather.11
  45.8 27.1 all-gather.9
  348.8 103.8 all-gather.5
  455.0 123.4 all-gather.7
where the time goes:
time: 918 us; the launch traced here: 911 us
  local copies, waits for them, and re-layouts  364 us (40%)
  waiting for transfers between devices  215 us (23%)
  blocking collectives  187 us (20%)
  other arithmetic  92.2 us (10%)
  matrix products  30.8 us (3%)
  between operations  13.6 us (1%)
    all_to_all x1, blocking collectives, shards(): lax.all_to_all(packed, 'row', split_axis=0, concat_axis=0, tiled=True)  187 us
    all_gather x1, waiting for transfers between devices, shards(): piece = lax.all_gather(parent_col, ('half', 'col'), axis=0, tiled=True)  124 us
    unnamed x31, local copies, waits for them, and re-layouts  113 us
    gather x6, local copies, waits for them, and re-layouts, shards(): jnp.take(picked, sibling * grid_size + col_source[sibling], axis=2)  89.1 us
    all_gather x1, waiting for transfers between devices, shards(): lax.all_gather(parent_row, 'row', axis=0, tiled=True)  57.6 us
    gather x5, local copies, waits for them, and re-layouts, shards(): picked = jnp.take(arrived, row_source[sibling], axis=0)  54.2 us
    select_n x3, other arithmetic, shards(): picked = jnp.take(arrived, row_source[sibling], axis=0)  45.3 us
    reshape x1, local copies, waits for them, and re-layouts, shards(): parent_front.reshape(2 * grid_size, tile_width, grid_size, tile_width)  34.4 us
  transfers between devices with their start and end apart: 5, of which 4 were waited for; matrix products, arithmetic and copies ran while one was open for 19% of the time, Pallas kernels for 0%

commit v1 on v0

v1 whole, which is shorter than its diff:
```python
import functools

import jax
import jax.numpy as jnp
from jax import lax
from jax.experimental import pallas as pl
from jax.experimental.pallas import tpu as pltpu
from jax.sharding import PartitionSpec as P

MESH = pl.DeviceIdType.MESH
T = 256
L = 128
G = 8
BF = jnp.bfloat16
F32 = jnp.float32

RELAYED = {
    (0, 0): (7,),
    (0, 1): (6, 7),
    (0, 3): (0, 1),
    (1, 1): (7,),
    (1, 2): (6, 7),
    (1, 3): (6, 7),
    (1, 7): (0, 1),
}
RELAYS = {}
for (_h, _c), _cols in RELAYED.items():
    for _v in _cols:
        RELAYS.setdefault((1 if _v < _c else 0, _c), []).append((_h, _v))
RELAY_SLOTS = max(len(v) for v in RELAYS.values())


def relay_route(h, c, target):
    relayed = h < 0
    slot = 0 * c
    for (hh, cc), cols in RELAYED.items():
        for v in cols:
            hit = (h == hh) & (c == cc) & (target == v)
            relayed = relayed | hit
            k = RELAYS[(1 if v < cc else 0, cc)].index((hh, v))
            if k:
                slot = jnp.where(hit, k, slot)
    return relayed, slot


def exchange_kernel(
    q_ref,
    block_hbm,
    crow_ref,
    ccol_ref,
    prow_ref,
    pcol_ref,
    cinv_ref,
    pinv_ref,
    recv_hbm,
    v_ref,
    pcol_hbm,
    stage,
    tile,
    plain,
    rowg,
    colg,
    colt,
    w,
    sbuf,
    lbuf,
    prowg,
    stage_sem,
    row_sem,
    col_sem,
    prow_sem,
    pcol_sem,
    ssem,
    rsem,
    lsem,
    fsem,
):
    h = lax.axis_index("half")
    r = lax.axis_index("row")
    c = lax.axis_index("col")
    slot_me = h * G + c

    def remote(src, dst, send, recv, dev):
        return pltpu.make_async_remote_copy(
            src_ref=src,
            dst_ref=dst,
            send_sem=send,
            recv_sem=recv,
            device_id=dev,
            device_id_type=MESH,
        )

    def fetch(k, s):
        return pltpu.make_async_copy(block_hbm.at[k], stage.at[s], stage_sem.at[s])

    fetch(0, 0).start()

    barrier = pltpu.get_barrier_semaphore()
    me = h * 64 + r * 8 + c

    def greet(i, _):
        @pl.when(i != me)
        def _():
            pl.semaphore_signal(
                barrier,
                inc=1,
                device_id=(i // 64, (i // 8) % 8, i % 8),
                device_id_type=MESH,
            )

        return 0

    lax.fori_loop(0, 128, greet, 0)
    pl.semaphore_wait(barrier, 127)

    row_part = pl.ds(pl.multiple_of(r * 32, 32), 32)
    col_part = pl.ds(pl.multiple_of(c * 32, 32), 32)
    pcol_part = pl.ds(pl.multiple_of(slot_me * 16, 16), 16)

    def send_child(t, _):
        remote(
            crow_ref, rowg.at[:, row_part, :], row_sem.at[0], row_sem.at[1], (h, (r + t) % G, c)
        ).start()
        remote(
            ccol_ref, colg.at[:, col_part, :], col_sem.at[0], col_sem.at[1], (h, r, (c + t) % G)
        ).start()
        return 0

    lax.fori_loop(1, G, send_child, 0)
    pltpu.make_async_copy(crow_ref, rowg.at[:, row_part, :], row_sem.at[1]).start()
    pltpu.make_async_copy(ccol_ref, colg.at[:, col_part, :], col_sem.at[1]).start()

    def send_prow(t, _):
        remote(
            prow_ref, prowg.at[:, row_part, :], prow_sem.at[0], prow_sem.at[1], (h, (r + t) % G, c)
        ).start()
        return 0

    lax.fori_loop(1, G, send_prow, 0)
    pltpu.make_async_copy(prow_ref, prowg.at[:, row_part, :], prow_sem.at[1]).start()

    def send_pcol(t, _):
        to = (slot_me + t) % (2 * G)
        remote(
            pcol_ref,
            pcol_hbm.at[:, pcol_part, :],
            pcol_sem.at[0],
            pcol_sem.at[1],
            (to // G, r, to % G),
        ).start()
        return 0

    lax.fori_loop(1, 2 * G, send_pcol, 0)
    pltpu.make_async_copy(pcol_ref, pcol_hbm.at[:, pcol_part, :], pcol_sem.at[1]).start()

    def split(k, _):
        s = k % 2

        @pl.when(k + 1 < G)
        def _():
            fetch(k + 1, 1 - s).start()

        fetch(k, s).wait()

        def widen(m, _):
            x = stage[s, pl.ds(pl.multiple_of(m * 32, 32), 32)]
            x = x.astype(F32).reshape(256, T)
            for lane in range(2):
                tile[lane, pl.ds(pl.multiple_of(m * 256, 256), 256), :] = x[:, lane * L : lane * L + L]
            return 0

        lax.fori_loop(0, 8, widen, 0)
        for kk in range(G):
            for lane in range(2):
                plain[k * G + kk, :, pl.ds(lane * L, L)] = tile[
                    lane, pl.ds(kk, T, stride=G), :
                ].astype(BF)
        return 0

    lax.fori_loop(0, G, split, 0)

    remote(rowg, rowg, row_sem.at[0], row_sem.at[1], (h, r, c)).wait_recv()

    def scale(k, _):
        w[k] = jnp.dot(cinv_ref[...], rowg[k], preferred_element_type=F32).astype(BF)
        return 0

    lax.fori_loop(0, G, scale, 0)
    remote(colg, colg, col_sem.at[0], col_sem.at[1], (h, r, c)).wait_recv()

    def turn(k, _):
        colt[k] = colg[k].T
        return 0

    lax.fori_loop(0, G, turn, 0)

    def block(i, _):
        d = (i // G + c) % G
        dd = (i + r) % G
        s = d * G + dd
        update = jnp.dot(colt[d], w[dd], preferred_element_type=F32)
        sbuf[s] = (plain[q_ref[d] * G + q_ref[dd]].astype(F32) - update).astype(BF)
        to = c + dd
        th, tr, tc = to // G, (r + d) % G, to % G
        relayed, slot = relay_route(h, c, tc)
        relayed = relayed & ((th != h) | (tr != r))
        here = (d == 0) & (to == slot_me)
        sent = jnp.where(s == 0, G, d)

        @pl.when(relayed)
        def _():
            remote(
                sbuf.at[s],
                lbuf.at[slot * G + r],
                ssem.at[sent],
                lsem.at[slot * G + r],
                (th, tr, c),
            ).start()

        @pl.when(jnp.logical_not(relayed | here))
        def _():
            remote(
                sbuf.at[s], recv_hbm.at[h, r, c], ssem.at[sent], rsem.at[h * G + c], (th, tr, tc)
            ).start()

        @pl.when(here)
        def _():
            pltpu.make_async_copy(sbuf.at[s], recv_hbm.at[h, r, c], rsem.at[h * G + c]).start()

        return 0

    lax.fori_loop(0, G * G, block, 0)

    for (rh, rc), passing in RELAYS.items():

        @pl.when((h == rh) & (c == rc))
        def _(rh=rh, passing=passing):
            def forward(i, _):
                d = (i + c) % G
                frm = (r - d + G) % G
                for slot, (hs, tc) in enumerate(passing):

                    def pass_on(slot=slot, hs=hs, tc=tc):
                        buf = lbuf.at[slot * G + frm]
                        remote(
                            buf, buf, fsem.at[slot], lsem.at[slot * G + frm], (1 - h, r, c)
                        ).wait_recv()
                        remote(
                            buf,
                            recv_hbm.at[hs, frm, c],
                            fsem.at[slot],
                            rsem.at[hs * G + c],
                            (h, r, tc),
                        ).start()

                    if hs == rh:
                        pl.when(d != 0)(pass_on)
                    else:
                        pass_on()
                return 0

            lax.fori_loop(0, G, forward, 0)

    remote(prowg, prowg, prow_sem.at[0], prow_sem.at[1], (h, r, c)).wait_recv()

    def pscale(k, _):
        v_ref[k] = jnp.dot(pinv_ref[...], prowg[k], preferred_element_type=F32).astype(BF)
        return 0

    lax.fori_loop(0, G, pscale, 0)

    seven = pl.ds(0, 7)
    other = (1 - h, r, c)
    remote(rowg.at[seven], rowg.at[seven], row_sem.at[0], row_sem.at[1], other).wait_send()
    remote(colg.at[seven], colg.at[seven], col_sem.at[0], col_sem.at[1], other).wait_send()
    remote(prowg.at[seven], prowg.at[seven], prow_sem.at[0], prow_sem.at[1], other).wait_send()
    fifteen = pl.ds(0, 15)
    remote(
        pcol_hbm.at[fifteen], pcol_hbm.at[fifteen], pcol_sem.at[0], pcol_sem.at[1], other
    ).wait_send()
    remote(pcol_hbm, pcol_hbm, pcol_sem.at[0], pcol_sem.at[1], other).wait_recv()

    for (rh, rc), passing in RELAYS.items():

        @pl.when((h == rh) & (c == rc))
        def _(rh=rh, passing=passing):
            for slot, (hs, _tc) in enumerate(passing):
                part = lbuf.at[pl.ds(0, G - 1 if hs == rh else G)]
                remote(part, part, fsem.at[slot], lsem.at[0], other).wait_send()

    part = sbuf.at[pl.ds(0, G - 1)]
    remote(part, part, ssem.at[0], rsem.at[0], other).wait_send()

    @pl.when(h == 1)
    def _():
        one = sbuf.at[pl.ds(0, 1)]
        remote(one, one, ssem.at[G], rsem.at[0], other).wait_send()

    for d in range(1, G):
        part = sbuf.at[pl.ds(0, G)]
        remote(part, part, ssem.at[d], rsem.at[0], other).wait_send()

    for hs in range(2):
        for cs in range(G):

            @pl.when((slot_me - cs >= 0) & (slot_me - cs < G))
            def _(hs=hs, cs=cs):
                dst = recv_hbm.at[hs, :, cs]
                remote(sbuf.at[pl.ds(0, G)], dst, ssem.at[0], rsem.at[hs * G + cs], other).wait_recv()


def exchange(q, block, crow, ccol, prow, pcol, cinv, pinv):
    any_space = pl.BlockSpec(memory_space=pl.ANY)
    vmem = pl.BlockSpec(memory_space=pltpu.VMEM)
    smem = pl.BlockSpec(memory_space=pltpu.SMEM)
    dma = pltpu.SemaphoreType.DMA
    return pl.pallas_call(
        exchange_kernel,
        out_shape=(
            jax.ShapeDtypeStruct((2, G, G, T, T), BF),
            jax.ShapeDtypeStruct((G, T, T), BF),
            jax.ShapeDtypeStruct((2 * G, T, T), BF),
        ),
        in_specs=[smem, any_space] + [vmem] * 6,
        out_specs=(any_space, vmem, any_space),
        scratch_shapes=[
            pltpu.VMEM((2, T, G, T), BF),
            pltpu.VMEM((2, T * G, L), F32),
            pltpu.VMEM((G * G, T, T), BF),
            pltpu.VMEM((G, T, T), BF),
            pltpu.VMEM((G, T, T), BF),
            pltpu.VMEM((G, T, T), BF),
            pltpu.VMEM((G, T, T), BF),
            pltpu.VMEM((G * G, T, T), BF),
            pltpu.VMEM((RELAY_SLOTS * G, T, T), BF),
            pltpu.VMEM((G, T, T), BF),
            dma((2,)),
            dma((2,)),
            dma((2,)),
            dma((2,)),
            dma((2,)),
            dma((G + 1,)),
            dma((2 * G,)),
            dma((RELAY_SLOTS * G,)),
            dma((RELAY_SLOTS,)),
        ],
        compiler_params=pltpu.CompilerParams(
            collective_id=0, has_side_effects=True, vmem_limit_bytes=48 << 20
        ),
        name="exchange",
    )(q, block, crow, ccol, prow, pcol, cinv, pinv)


def assemble_kernel(
    rows_ref, cols_ref, info_ref, from0, from1, v_ref, pcol_ref, diag_ref, out_ref, tile
):
    k = pl.program_id(0)
    odd = pl.program_id(1)
    pc = pcol_ref[0]
    for b in range(G):
        acc = -lax.dot_general(
            pc, v_ref[b], (((0,), (0,)), ((), ())), preferred_element_type=F32
        )
        for hs, part in ((0, from0), (1, from1)):
            cs = cols_ref[hs * G + b]
            live = (info_ref[2 * G + hs * G + k] == odd) & (cs >= 0) & (cs < G)
            piece = part[0, 0, jnp.clip(cs, 0, G - 1)].astype(F32)
            acc = acc + jnp.where(live, piece, 0.0)
        for lane in range(2):
            tile[lane, pl.ds(b, T, stride=G), :] = acc[:, lane * L : lane * L + L]

    @pl.when((info_ref[0] == 1) & (info_ref[1] == odd))
    def _():
        i = lax.broadcasted_iota(jnp.int32, (T, T), 0)
        j = lax.broadcasted_iota(jnp.int32, (T, T), 1)
        extra = jnp.where(i == j, diag_ref[0], 0.0)
        for b in range(G):

            @pl.when(k == b)
            def _():
                for lane in range(2):
                    tile[lane, pl.ds(b, T, stride=G), :] += extra[:, lane * L : lane * L + L]

    for m in range(8):
        for lane in range(2):
            out_ref[0, pl.ds(m * 32, 32), :, pl.ds(lane * L, L)] = (
                tile[lane, pl.ds(m * 256, 256), :].reshape(32, G, L).astype(BF)
            )


def assemble(rows, cols, info, recv, v, pcol, diag):
    whole = pl.BlockSpec((G, T, T), lambda k, o, *_: (0, 0, 0))
    return pl.pallas_call(
        assemble_kernel,
        out_shape=jax.ShapeDtypeStruct((2 * G, T, G, T), BF),
        grid_spec=pltpu.PrefetchScalarGridSpec(
            num_scalar_prefetch=3,
            grid=(G, 2),
            in_specs=[
                pl.BlockSpec((1, 1, G, T, T), lambda k, o, rows, *_: (0, rows[k], 0, 0, 0)),
                pl.BlockSpec((1, 1, G, T, T), lambda k, o, rows, *_: (1, rows[G + k], 0, 0, 0)),
                whole,
                pl.BlockSpec((1, T, T), lambda k, o, *_: (2 * k + o, 0, 0)),
                pl.BlockSpec((1, 1, T), lambda k, o, *_: (2 * k + o, 0, 0)),
            ],
            out_specs=pl.BlockSpec((1, T, G, T), lambda k, o, *_: (2 * k + o, 0, 0, 0)),
            scratch_shapes=[pltpu.VMEM((2, T * G, L), F32)],
        ),
        compiler_params=pltpu.CompilerParams(vmem_limit_bytes=48 << 20),
        name="assemble",
    )(rows, cols, info, recv, recv, v, pcol, diag)


def shards(
    child_block,
    child_row,
    child_col,
    child_pivot_inv,
    child_map,
    parent_row,
    parent_col,
    parent_pivot_inv,
    parent_diag,
):
    h = lax.axis_index("half")
    r = lax.axis_index("row")
    c = lax.axis_index("col")
    steps = jnp.arange(G, dtype=jnp.int32)
    shift = child_map.reshape(2, G, G)[:, :, 0] - 2 * G * steps[None, :]
    source = jnp.sum(
        jnp.where(shift[:, None, :] == steps[None, :, None], steps[None, None, :], 0), axis=2
    ).astype(jnp.int32)
    q = lax.dynamic_index_in_dim(source, h, 0, keepdims=False)

    def ordered(x):
        x = x.reshape(x.shape[1], G, T)
        return jnp.swapaxes(jnp.take(x, q, axis=1), 0, 1)

    crow = ordered(child_row)
    ccol = ordered(child_col)
    prow = jnp.swapaxes(parent_row.reshape(-1, G, T), 0, 1)
    pcol = jnp.swapaxes(parent_col.reshape(-1, 2 * G, T), 0, 1)
    recv, v, pcols = exchange(
        q,
        child_block.reshape(G, T, G, T),
        crow,
        ccol,
        prow,
        pcol,
        child_pivot_inv[0],
        parent_pivot_inv,
    )
    rows = ((r - shift) % G).reshape(-1)
    cols = (h * G + c - shift).reshape(-1)
    carry = (shift > r).astype(jnp.int32).reshape(-1)
    head = jnp.stack([(r == c).astype(jnp.int32), h.astype(jnp.int32)])
    info = jnp.concatenate([head, jnp.zeros((2 * G - 2,), jnp.int32), carry])
    out = assemble(rows, cols, info, recv, v, pcols, parent_diag)
    return out.reshape(2 * G, 1, T, G, 1, T)


def solution(mesh):
    return jax.shard_map(
        shards,
        mesh=mesh,
        in_specs=(
            P("half", None, "row", None, None, "col", None),
            P("half", "row", None, "col", None),
            P("half", "col", None, "row", None),
            P("half", None, None),
            P(),
            P("row", None, ("half", "col"), None),
            P(("half", "col"), None, "row", None),
            P(),
            P(None, "row", None),
        ),
        out_specs=P(None, "row", None, None, ("half", "col"), None),
        check_vma=False,
    )
```

time: 918 us -> 284 us (0.31)
  local copies, waits for them, and re-layouts: 364 us -> 8.45 us
  Pallas kernels: 0 us -> 274 us
  waiting for transfers between devices: 215 us -> 0 us
  blocking collectives: 187 us -> 0 us
  other arithmetic: 92.2 us -> 0.38 us
  matrix products: 30.8 us -> 0 us
  between operations: 13.6 us -> 0.1 us
    pallas_call x0 -> x2, Pallas kernels: none -> 274 us  [the longest x1 248 us: exchange(): pl.pallas_call(exchange_kernel, out_shape=(jax.ShapeDtypeStruct((2, G, G,...]
    all_gather x4 -> x0, waiting for transfers between devices: 212 us -> none  [the longest x1 124 us: shards(): piece = lax.all_gather(parent_col, ('half', 'col'), axis=0, tiled=True)]
    all_to_all x1 -> x0, blocking collectives: 187 us -> none  [shards(): lax.all_to_all(packed, 'row', split_axis=0, concat_axis=0, tiled=True)]
    gather x19 -> x2, local copies, waits for them, and re-layouts: 164 us -> 1.11 us  [ordered(): return jnp.swapaxes(jnp.take(x, q, axis=1), 0, 1)]
    unnamed x31 -> x10, local copies, waits for them, and re-layouts: 113 us -> 6.26 us
    select_n x14 -> x2, other arithmetic: 62.2 us -> 0.1 us  [ordered(): return jnp.swapaxes(jnp.take(x, q, axis=1), 0, 1)]
    reshape x3 -> x1, local copies, waits for them, and re-layouts: 58.1 us -> 0.75 us  [shards(): shift = child_map.reshape(2, G, G)[:, :, 0] - 2 * G * steps[None, :]]
    dot_general x2 -> x0, matrix products: 30.8 us -> none  [shards(): lax.dot_general(flattened, scaled_part, (((0,), (0,)), ((), ())), preferr...]
  transfers between devices with their start and end apart: 5 -> 0, of which waited for: 4 -> 0; matrix products, arithmetic and copies ran while one was open for 19% -> 0% of each run, Pallas kernels for 0% -> 0%
where the time goes in v1:
time: 284 us; the launch traced here: 283 us
  Pallas kernels  274 us (96%)
  local copies, waits for them, and re-layouts  8.45 us (3%)
    pallas_call x1, Pallas kernels, exchange(): pl.pallas_call(exchange_kernel, out_shape=(jax.ShapeDtypeStruct((2, G, G,...  248 us
    pallas_call x1, Pallas kernels, assemble(): pl.pallas_call(assemble_kernel, out_shape=jax.ShapeDtypeStruct((2 * G, T,...  25.8 us
    unnamed x10, local copies, waits for them, and re-layouts  6.26 us

profile of v1, /device:TPU:15, one launch (start us, length us, event | category | flops | bytes accessed | tf_op | source)
XLA Modules:
  0.0 282.8 jit_solution(7379969020243868543)
XLA Ops:
  0.0 0.1 sub.37
  0.1 0.8 reshape.56
  0.8 0.1 slice_reduce_fusion
  1.0 0.1 squeeze.12
  1.1 0.2 select_reduce_fusion
  1.3 0.1 pad_add_fusion.info_ref
  1.4 0.9 copy.30
  2.3 0.6 gather_fusion
  2.9 0.9 copy.29
  3.8 0.6 gather_fusion.1
  4.4 0.1 broadcast_select_fusion
  4.5 0.9 copy.28
  5.4 0.9 copy.27
  6.4 0.0 copy-start
  6.4 0.9 copy-done
  7.3 0.0 copy-start.1
  7.3 0.9 copy-done.1
  8.2 248.0 %exchange.1 = (bf16[2,8,8,256,256]{4,3,2,1,0:T(8,128)(2,1)}, bf16[8,256,256]{2,1,0:T(8,128)(2,1)S(1)}, bf16[16,256,256]{2,1,0:T(8,128)(2,1)S(1)}) custom-call(s32[8]{0:T(128)S(1)} %get-tuple-element.13.q_ref, bf16[8,256,8,256]{3,2,1,0:T(8,128)(2,1)} %bitcast.35, bf16[8,32,256]{2,1,0:T(8,128)(2,1)S(1)} %get-tuple-element.17.crow_ref, ...), custom_call_target="tpu_custom_call" | custom-call | tf_op jit(solution)/shard_map/exchange/pallas_call | solution.py:317
  256.2 0.0 copy-start.2
  256.2 0.7 copy-done.2
  256.9 25.8 %assemble.1 = bf16[16,256,8,256]{3,2,1,0:T(8,128)(2,1)} custom-call(s32[16]{0:T(128)S(1)} %get-tuple-element.15.rows_ref, s32[16]{0:T(128)S(1)} %get-tuple-element.14.cols_ref, s32[32]{0:T(128)S(1)} %pad_add_fusion.info_ref, bf16[2,8,8,256,256]{4,3,2,1,0:T(8,128)(2,1)} %get-tuple-element.9.from0.from1, ...), custom_call_target="tpu_custom_call" | custom-call | tf_op jit(solution)/shard_map/assemble/pallas_call | solution.py:393
  (9 shorter events, 0.1 us)
Async XLA Ops:
  6.4 0.9 copy-start
  7.3 0.9 copy-start.1
  256.2 0.7 copy-start.2

commit v2 on v1

--- a/solution.py
+++ b/solution.py
@@ -41,6 +41,10 @@
             if k:
                 slot = jnp.where(hit, k, slot)
     return relayed, slot
+
+
+def turn_of(i):
+    return i % G, (2 * (i // G) + i // (4 * G) + i) % G
 
 
 def exchange_kernel(
@@ -65,6 +69,7 @@
     sbuf,
     lbuf,
     prowg,
+    zeros,
     stage_sem,
     row_sem,
     col_sem,
@@ -113,45 +118,54 @@
     lax.fori_loop(0, 128, greet, 0)
     pl.semaphore_wait(barrier, 127)
 
+    other = (1 - h, r, c)
+    pair = (h, (r + G // 2) % G, c)
+    twin = (h, r, c + 1 - 2 * (c % 2))
     row_part = pl.ds(pl.multiple_of(r * 32, 32), 32)
-    col_part = pl.ds(pl.multiple_of(c * 32, 32), 32)
-    pcol_part = pl.ds(pl.multiple_of(slot_me * 16, 16), 16)
-
-    def send_child(t, _):
-        remote(
-            crow_ref, rowg.at[:, row_part, :], row_sem.at[0], row_sem.at[1], (h, (r + t) % G, c)
-        ).start()
-        remote(
-            ccol_ref, colg.at[:, col_part, :], col_sem.at[0], col_sem.at[1], (h, r, (c + t) % G)
-        ).start()
-        return 0
-
-    lax.fori_loop(1, G, send_child, 0)
-    pltpu.make_async_copy(crow_ref, rowg.at[:, row_part, :], row_sem.at[1]).start()
-    pltpu.make_async_copy(ccol_ref, colg.at[:, col_part, :], col_sem.at[1]).start()
-
-    def send_prow(t, _):
-        remote(
-            prow_ref, prowg.at[:, row_part, :], prow_sem.at[0], prow_sem.at[1], (h, (r + t) % G, c)
-        ).start()
-        return 0
-
-    lax.fori_loop(1, G, send_prow, 0)
-    pltpu.make_async_copy(prow_ref, prowg.at[:, row_part, :], prow_sem.at[1]).start()
-
-    def send_pcol(t, _):
-        to = (slot_me + t) % (2 * G)
-        remote(
-            pcol_ref,
-            pcol_hbm.at[:, pcol_part, :],
-            pcol_sem.at[0],
-            pcol_sem.at[1],
-            (to // G, r, to % G),
-        ).start()
-        return 0
-
-    lax.fori_loop(1, 2 * G, send_pcol, 0)
-    pltpu.make_async_copy(pcol_ref, pcol_hbm.at[:, pcol_part, :], pcol_sem.at[1]).start()
+    pair_part = pl.ds(pl.multiple_of((r + G // 2) % G * 32, 32), 32)
+
+    def rows_out(panel, whole, sems):
+        remote(panel, whole.at[:, row_part, :], sems.at[0], sems.at[2], pair).start()
+        for t in range(1, 4):
+            to = (h, r // 4 * 4 + (r + t) % 4, c)
+            remote(panel, whole.at[:, row_part, :], sems.at[0], sems.at[3], to).start()
+        pltpu.make_async_copy(panel, whole.at[:, row_part, :], sems.at[3]).start()
+
+    def rows_on(whole, sems):
+        part = whole.at[:, pair_part, :]
+        remote(part, part, sems.at[0], sems.at[2], pair).wait_recv()
+        for t in range(1, 4):
+            to = (h, r // 4 * 4 + (r + t) % 4, c)
+            remote(part, part, sems.at[1], sems.at[4], to).start()
+
+    def rows_in(whole, sems):
+        four, three = whole.at[pl.ds(0, 4)], whole.at[pl.ds(0, 3)]
+        remote(four, four, sems.at[0], sems.at[3], pair).wait_recv()
+        remote(three, three, sems.at[0], sems.at[4], pair).wait_recv()
+
+    def rows_left(whole, sems):
+        four, three = whole.at[pl.ds(0, 4)], whole.at[pl.ds(0, 3)]
+        remote(four, four, sems.at[0], sems.at[3], pair).wait_send()
+        remote(three, three, sems.at[1], sems.at[4], pair).wait_send()
+
+    ccol_part = pl.ds(pl.multiple_of(c % 2 * 128 + c // 2 * 32, 32), 32)
+    ccol_core = pl.ds(pl.multiple_of(c % 2 * 128, 128), 128)
+    pcol_part = pl.ds(pl.multiple_of(c % 2 * 128 + h * 64 + c // 2 * 16, 16), 16)
+    pcol_over = pl.ds(pl.multiple_of(c % 2 * 128 + (1 - h) * 64 + c // 2 * 16, 16), 16)
+    pcol_core = pl.ds(pl.multiple_of(c % 2 * 128, 128), 128)
+
+    rows_out(crow_ref, rowg, row_sem)
+    for t in range(1, 4):
+        to = (h, r, (c + 2 * t) % G)
+        remote(ccol_ref, colg.at[:, ccol_part, :], col_sem.at[0], col_sem.at[2], to).start()
+    pltpu.make_async_copy(ccol_ref, colg.at[:, ccol_part, :], col_sem.at[2]).start()
+    remote(pcol_ref, pcol_hbm.at[:, pcol_part, :], pcol_sem.at[0], pcol_sem.at[3], other).start()
+    rows_out(prow_ref, prowg, prow_sem)
+    for t in range(1, 4):
+        to = (h, r, (c + 2 * t) % G)
+        remote(pcol_ref, pcol_hbm.at[:, pcol_part, :], pcol_sem.at[0], pcol_sem.at[4], to).start()
+    pltpu.make_async_copy(pcol_ref, pcol_hbm.at[:, pcol_part, :], pcol_sem.at[4]).start()
+    rows_on(rowg, row_sem)
 
     def split(k, _):
         s = k % 2
@@ -179,14 +193,25 @@
 
     lax.fori_loop(0, G, split, 0)
 
-    remote(rowg, rowg, row_sem.at[0], row_sem.at[1], (h, r, c)).wait_recv()
+    zeros[...] = jnp.zeros_like(zeros)
+    half_part = colg.at[:, ccol_core, :]
+    remote(half_part, half_part, col_sem.at[0], col_sem.at[2], twin).wait_recv()
+    remote(half_part, half_part, col_sem.at[1], col_sem.at[3], twin).start()
+    rows_on(prowg, prow_sem)
+    part = pcol_hbm.at[:, pcol_over, :]
+    remote(part, part, pcol_sem.at[0], pcol_sem.at[3], other).wait_recv()
+    for t in range(1, 4):
+        to = (h, r, (c + 2 * t) % G)
+        remote(part, part, pcol_sem.at[1], pcol_sem.at[5], to).start()
+
+    rows_in(rowg, row_sem)
 
     def scale(k, _):
         w[k] = jnp.dot(cinv_ref[...], rowg[k], preferred_element_type=F32).astype(BF)
         return 0
 
     lax.fori_loop(0, G, scale, 0)
-    remote(colg, colg, col_sem.at[0], col_sem.at[1], (h, r, c)).wait_recv()
+    remote(half_part, half_part, col_sem.at[1], col_sem.at[3], twin).wait_recv()
 
     def turn(k, _):
         colt[k] = colg[k].T
@@ -195,8 +220,7 @@
     lax.fori_loop(0, G, turn, 0)
 
     def block(i, _):
-        d = (i // G + c) % G
-        dd = (i + r) % G
+        d, dd = turn_of(i)
         s = d * G + dd
         update = jnp.dot(colt[d], w[dd], preferred_element_type=F32)
         sbuf[s] = (plain[q_ref[d] * G + q_ref[dd]].astype(F32) - update).astype(BF)
@@ -231,16 +255,34 @@
 
     lax.fori_loop(0, G * G, block, 0)
 
+    four = pcol_hbm.at[pl.ds(0, 4)]
+    three = pcol_hbm.at[pl.ds(0, 3)]
+    remote(four, four, pcol_sem.at[0], pcol_sem.at[4], other).wait_recv()
+    remote(three, three, pcol_sem.at[0], pcol_sem.at[5], other).wait_recv()
+    part = pcol_hbm.at[:, pcol_core, :]
+    remote(part, part, pcol_sem.at[2], pcol_sem.at[6], twin).start()
+
+    for hs in range(2):
+        for cs in range(G):
+
+            @pl.when((slot_me - cs < 0) | (slot_me - cs >= G))
+            def _(hs=hs, cs=cs):
+                pltpu.make_async_copy(zeros, recv_hbm.at[hs, :, cs], rsem.at[hs * G + cs]).start()
+
     for (rh, rc), passing in RELAYS.items():
 
         @pl.when((h == rh) & (c == rc))
-        def _(rh=rh, passing=passing):
+        def _(rh=rh, rc=rc, passing=passing):
             def forward(i, _):
-                d = (i + c) % G
+                d, dd = turn_of(i)
                 frm = (r - d + G) % G
                 for slot, (hs, tc) in enumerate(passing):
-
-                    def pass_on(slot=slot, hs=hs, tc=tc):
+                    due = dd == (tc - rc) % G
+                    if hs == rh:
+                        due = due & (d != 0)
+
+                    @pl.when(due)
+                    def _(slot=slot, hs=hs, tc=tc):
                         buf = lbuf.at[slot * G + frm]
                         remote(
                             buf, buf, fsem.at[slot], lsem.at[slot * G + frm], (1 - h, r, c)
@@ -253,32 +295,28 @@
                             (h, r, tc),
                         ).start()
 
-                    if hs == rh:
-                        pl.when(d != 0)(pass_on)
-                    else:
-                        pass_on()
                 return 0
 
-            lax.fori_loop(0, G, forward, 0)
-
-    remote(prowg, prowg, prow_sem.at[0], prow_sem.at[1], (h, r, c)).wait_recv()
+            lax.fori_loop(0, G * G, forward, 0)
+
+    rows_in(prowg, prow_sem)
 
     def pscale(k, _):
-        v_ref[k] = jnp.dot(pinv_ref[...], prowg[k], preferred_element_type=F32).astype(BF)
+        v_ref[k] = -jnp.dot(pinv_ref[...], prowg[k], preferred_element_type=F32).astype(BF)
         return 0
 
     lax.fori_loop(0, G, pscale, 0)
 
-    seven = pl.ds(0, 7)
-    other = (1 - h, r, c)
-    remote(rowg.at[seven], rowg.at[seven], row_sem.at[0], row_sem.at[1], other).wait_send()
-    remote(colg.at[seven], colg.at[seven], col_sem.at[0], col_sem.at[1], other).wait_send()
-    remote(prowg.at[seven], prowg.at[seven], prow_sem.at[0], prow_sem.at[1], other).wait_send()
-    fifteen = pl.ds(0, 15)
-    remote(
-        pcol_hbm.at[fifteen], pcol_hbm.at[fifteen], pcol_sem.at[0], pcol_sem.at[1], other
-    ).wait_send()
-    remote(pcol_hbm, pcol_hbm, pcol_sem.at[0], pcol_sem.at[1], other).wait_recv()
+    rows_left(rowg, row_sem)
+    rows_left(prowg, prow_sem)
+    quarter = colg.at[:, pl.ds(0, 96), :]
+    remote(quarter, quarter, col_sem.at[0], col_sem.at[2], twin).wait_send()
+    remote(half_part, half_part, col_sem.at[1], col_sem.at[3], twin).wait_send()
+    remote(four, four, pcol_sem.at[0], pcol_sem.at[3], twin).wait_send()
+    remote(three, three, pcol_sem.at[1], pcol_sem.at[3], twin).wait_send()
+    part = pcol_hbm.at[:, pcol_core, :]
+    remote(part, part, pcol_sem.at[2], pcol_sem.at[6], twin).wait_send()
+    remote(part, part, pcol_sem.at[2], pcol_sem.at[6], twin).wait_recv()
 
     for (rh, rc), passing in RELAYS.items():
 
@@ -302,11 +340,8 @@
 
     for hs in range(2):
         for cs in range(G):
-
-            @pl.when((slot_me - cs >= 0) & (slot_me - cs < G))
-            def _(hs=hs, cs=cs):
-                dst = recv_hbm.at[hs, :, cs]
-                remote(sbuf.at[pl.ds(0, G)], dst, ssem.at[0], rsem.at[hs * G + cs], other).wait_recv()
+            dst = recv_hbm.at[hs, :, cs]
+            remote(sbuf.at[pl.ds(0, G)], dst, ssem.at[0], rsem.at[hs * G + cs], other).wait_recv()
 
 
 def exchange(q, block, crow, ccol, prow, pcol, cinv, pinv):
@@ -317,9 +352,9 @@
     return pl.pallas_call(
         exchange_kernel,
         out_shape=(
-            jax.ShapeDtypeStruct((2, G, G, T, T), BF),
-            jax.ShapeDtypeStruct((G, T, T), BF),
-            jax.ShapeDtypeStruct((2 * G, T, T), BF),
+            pltpu.VMEM((2, G, G, T, T), BF),
+            pltpu.VMEM((G, T, T), BF),
+            pltpu.VMEM((2 * G, T, T), BF),
         ),
         in_specs=[smem, any_space] + [vmem] * 6,
         out_specs=(any_space, vmem, any_space),
@@ -334,52 +369,52 @@
             pltpu.VMEM((G * G, T, T), BF),
             pltpu.VMEM((RELAY_SLOTS * G, T, T), BF),
             pltpu.VMEM((G, T, T), BF),
+            pltpu.VMEM((G, T, T), BF),
             dma((2,)),
-            dma((2,)),
-            dma((2,)),
-            dma((2,)),
-            dma((2,)),
+            dma((5,)),
+            dma((4,)),
+            dma((5,)),
+            dma((7,)),
             dma((G + 1,)),
             dma((2 * G,)),
             dma((RELAY_SLOTS * G,)),
             dma((RELAY_SLOTS,)),
         ],
         compiler_params=pltpu.CompilerParams(
-            collective_id=0, has_side_effects=True, vmem_limit_bytes=48 << 20
+            collective_id=0, has_side_effects=True, vmem_limit_bytes=34 << 20
         ),
         name="exchange",
     )(q, block, crow, ccol, prow, pcol, cinv, pinv)
 
 
 def assemble_kernel(
-    rows_ref, cols_ref, info_ref, from0, from1, v_ref, pcol_ref, diag_ref, out_ref, tile
+    rows_ref, cols_ref, info_ref, recv_ref, v_ref, pcol_ref, diag_ref, out_ref, tile
 ):
     k = pl.program_id(0)
     odd = pl.program_id(1)
-    pc = pcol_ref[0]
-    for b in range(G):
-        acc = -lax.dot_general(
-            pc, v_ref[b], (((0,), (0,)), ((), ())), preferred_element_type=F32
-        )
-        for hs, part in ((0, from0), (1, from1)):
-            cs = cols_ref[hs * G + b]
-            live = (info_ref[2 * G + hs * G + k] == odd) & (cs >= 0) & (cs < G)
-            piece = part[0, 0, jnp.clip(cs, 0, G - 1)].astype(F32)
-            acc = acc + jnp.where(live, piece, 0.0)
-        for lane in range(2):
-            tile[lane, pl.ds(b, T, stride=G), :] = acc[:, lane * L : lane * L + L]
+    live = [info_ref[2 + hs * G + k] == odd for hs in range(2)]
+
+    def fill(parts):
+        pc = pcol_ref[0].T
+        for b in range(G):
+            acc = jnp.dot(pc, v_ref[b], preferred_element_type=F32)
+            for hs in parts:
+                acc = acc + recv_ref[hs, rows_ref[hs * G + k], cols_ref[hs * G + b]].astype(F32)
+            for lane in range(2):
+                tile[lane, pl.ds(b, T, stride=G), :] = acc[:, lane * L : lane * L + L]
+
+    pl.when(live[0] & live[1])(lambda: fill((0, 1)))
+    pl.when(live[0] & jnp.logical_not(live[1]))(lambda: fill((0,)))
+    pl.when(live[1] & jnp.logical_not(live[0]))(lambda: fill((1,)))
+    pl.when(jnp.logical_not(live[0] | live[1]))(lambda: fill(()))
 
     @pl.when((info_ref[0] == 1) & (info_ref[1] == odd))
     def _():
         i = lax.broadcasted_iota(jnp.int32, (T, T), 0)
         j = lax.broadcasted_iota(jnp.int32, (T, T), 1)
         extra = jnp.where(i == j, diag_ref[0], 0.0)
-        for b in range(G):
-
-            @pl.when(k == b)
-            def _():
-                for lane in range(2):
-                    tile[lane, pl.ds(b, T, stride=G), :] += extra[:, lane * L : lane * L + L]
+        for lane in range(2):
+            tile[lane, pl.ds(k, T, stride=G), :] += extra[:, lane * L : lane * L + L]
 
     for m in range(8):
         for lane in range(2):
@@ -390,6 +425,7 @@
 
 def assemble(rows, cols, info, recv, v, pcol, diag):
     whole = pl.BlockSpec((G, T, T), lambda k, o, *_: (0, 0, 0))
+    recv, v, pcol = (pltpu.with_memory_space_constraint(x, pltpu.VMEM) for x in (recv, v, pcol))
     return pl.pallas_call(
         assemble_kernel,
         out_shape=jax.ShapeDtypeStruct((2 * G, T, G, T), BF),
@@ -397,8 +433,7 @@
             num_scalar_prefetch=3,
             grid=(G, 2),
             in_specs=[
-                pl.BlockSpec((1, 1, G, T, T), lambda k, o, rows, *_: (0, rows[k], 0, 0, 0)),
-                pl.BlockSpec((1, 1, G, T, T), lambda k, o, rows, *_: (1, rows[G + k], 0, 0, 0)),
+                pl.BlockSpec(memory_space=pltpu.VMEM),
                 whole,
                 pl.BlockSpec((1, T, T), lambda k, o, *_: (2 * k + o, 0, 0)),
                 pl.BlockSpec((1, 1, T), lambda k, o, *_: (2 * k + o, 0, 0)),
@@ -406,9 +441,9 @@
             out_specs=pl.BlockSpec((1, T, G, T), lambda k, o, *_: (2 * k + o, 0, 0, 0)),
             scratch_shapes=[pltpu.VMEM((2, T * G, L), F32)],
         ),
-        compiler_params=pltpu.CompilerParams(vmem_limit_bytes=48 << 20),
+        compiler_params=pltpu.CompilerParams(vmem_limit_bytes=12 << 20),
         name="assemble",
-    )(rows, cols, info, recv, recv, v, pcol, diag)
+    )(rows, cols, info, recv, v, pcol, diag)
 
 
 def shards(
@@ -440,21 +475,16 @@
     ccol = ordered(child_col)
     prow = jnp.swapaxes(parent_row.reshape(-1, G, T), 0, 1)
     pcol = jnp.swapaxes(parent_col.reshape(-1, 2 * G, T), 0, 1)
+    cinv = jnp.swapaxes(child_pivot_inv.reshape(4, 2, 32, T), 0, 1).reshape(T, T)
+    pinv = jnp.transpose(parent_pivot_inv.reshape(2, 4, 2, 16, T), (2, 0, 1, 3, 4)).reshape(T, T)
     recv, v, pcols = exchange(
-        q,
-        child_block.reshape(G, T, G, T),
-        crow,
-        ccol,
-        prow,
-        pcol,
-        child_pivot_inv[0],
-        parent_pivot_inv,
+        q, child_block.reshape(G, T, G, T), crow, ccol, prow, pcol, cinv, pinv
     )
     rows = ((r - shift) % G).reshape(-1)
-    cols = (h * G + c - shift).reshape(-1)
+    cols = ((c - shift) % G).reshape(-1)
     carry = (shift > r).astype(jnp.int32).reshape(-1)
     head = jnp.stack([(r == c).astype(jnp.int32), h.astype(jnp.int32)])
-    info = jnp.concatenate([head, jnp.zeros((2 * G - 2,), jnp.int32), carry])
+    info = jnp.concatenate([head, carry])
     out = assemble(rows, cols, info, recv, v, pcols, parent_diag)
     return out.reshape(2 * G, 1, T, G, 1, T)
 

time: 284 us -> 232 us (0.82)
  the two profiles are of different devices: /device:TPU:15 before, /device:TPU:39 now
where the time goes in v2:
time: 232 us
  Pallas kernels  223 us (96%)
  local copies, waits for them, and re-layouts  8.47 us (4%)
    pallas_call x1, Pallas kernels, exchange(): pl.pallas_call(exchange_kernel, out_shape=(pltpu.VMEM((2, G, G, T, T), BF...  208 us
    pallas_call x1, Pallas kernels, assemble(): pl.pallas_call(assemble_kernel, out_shape=jax.ShapeDtypeStruct((2 * G, T,...  15.1 us

profile of v2, /device:TPU:39, one launch (start us, length us, event | category | flops | bytes accessed | tf_op | source)
XLA Modules:
  0.0 232.1 jit_solution(3756422793560903210)
XLA Ops:
  0.0 0.1 sub.37
  0.1 0.8 reshape.68
  0.8 0.1 slice_reduce_fusion
  1.0 0.1 squeeze.9
  1.1 0.2 select_reduce_fusion
  1.3 0.1 pad_add_fusion.info_ref
  1.4 0.9 copy.36
  2.3 0.6 gather_fusion
  2.9 0.9 copy.35
  3.8 0.6 gather_fusion.1
  4.4 0.1 broadcast_select_fusion
  4.5 0.9 copy.26
  5.4 0.9 copy.34
  6.3 0.9 copy.33
  7.3 0.9 copy.27
  8.2 208.1 %exchange.1 = (bf16[2,8,8,256,256]{4,3,2,1,0:T(8,128)(2,1)S(1)}, bf16[8,256,256]{2,1,0:T(8,128)(2,1)S(1)}, bf16[16,256,256]{2,1,0:T(8,128)(2,1)S(1)}) custom-call(s32[8]{0:T(128)S(1)} %get-tuple-element.13.q_ref, bf16[8,256,8,256]{3,2,1,0:T(8,128)(2,1)} %bitcast.43, bf16[8,32,256]{2,1,0:T(8,128)(2,1)S(1)} %get-tuple-element.17.crow_ref, ...), custom_call_target="tpu_custom_call" | custom-call | tf_op jit(solution)/shard_map/exchange/pallas_call | solution.py:352
  216.3 0.0 copy-start
  216.3 0.7 copy-done
  217.0 15.1 %assemble.1 = bf16[16,256,8,256]{3,2,1,0:T(8,128)(2,1)} custom-call(s32[16]{0:T(128)S(1)} %get-tuple-element.15.rows_ref, s32[16]{0:T(128)S(1)} %get-tuple-element.14.cols_ref, s32[18]{0:T(128)S(1)} %pad_add_fusion.info_ref, bf16[2,8,8,256,256]{4,3,2,1,0:T(8,128)(2,1)S(1)} %get-tuple-element.9.recv_ref, bf16[8,256,256]{2,1,0:T(8,128)(2,1)S(1)} %get-tuple-element.10.v_ref, ...), custom_call_target="tpu_custom_call" | custom-call | tf_op jit(solution)/shard_map/assemble/pallas_call | solution.py:429
  (8 shorter events, 0.1 us)
Async XLA Ops:
  216.3 0.7 copy-start

commit v3 on v2

--- a/solution.py
+++ b/solution.py
@@ -15,13 +15,20 @@
 F32 = jnp.float32
 
 RELAYED = {
-    (0, 0): (7,),
-    (0, 1): (6, 7),
-    (0, 3): (0, 1),
-    (1, 1): (7,),
-    (1, 2): (6, 7),
-    (1, 3): (6, 7),
-    (1, 7): (0, 1),
+    (0, 0): (2, 6, 7),
+    (0, 1): (4, 6, 7),
+    (0, 2): (0, 7),
+    (0, 3): (1, 4, 7),
+    (0, 5): (3,),
+    (0, 6): (0, 3),
+    (0, 7): (0,),
+    (1, 0): (7,),
+    (1, 1): (5, 7),
+    (1, 2): (6,),
+    (1, 3): (5,),
+    (1, 4): (0, 1, 6),
+    (1, 6): (1, 3),
+    (1, 7): (0, 1, 2),
 }
 RELAYS = {}
 for (_h, _c), _cols in RELAYED.items():
@@ -44,7 +51,7 @@
 
 
 def turn_of(i):
-    return i % G, (2 * (i // G) + i // (4 * G) + i) % G
+    return 3 * i % G, (2 * (i // G) + i // (4 * G) + i) % G
 
 
 def exchange_kernel(
@@ -220,10 +227,8 @@
     lax.fori_loop(0, G, turn, 0)
 
     def block(i, _):
-        d, dd = turn_of(i)
+        d, dd = turn_of(i % (G * G))
         s = d * G + dd
-        update = jnp.dot(colt[d], w[dd], preferred_element_type=F32)
-        sbuf[s] = (plain[q_ref[d] * G + q_ref[dd]].astype(F32) - update).astype(BF)
         to = c + dd
         th, tr, tc = to // G, (r + d) % G, to % G
         relayed, slot = relay_route(h, c, tc)
@@ -231,8 +236,13 @@
         here = (d == 0) & (to == slot_me)
         sent = jnp.where(s == 0, G, d)
 
-        @pl.when(relayed)
+        def make():
+            update = jnp.dot(colt[d], w[dd], preferred_element_type=F32)
+            sbuf[s] = (plain[q_ref[d] * G + q_ref[dd]].astype(F32) - update).astype(BF)
+
+        @pl.when(relayed & (i < G * G))
         def _():
+            make()
             remote(
                 sbuf.at[s],
                 lbuf.at[slot * G + r],
@@ -241,19 +251,27 @@
                 (th, tr, c),
             ).start()
 
-        @pl.when(jnp.logical_not(relayed | here))
+        @pl.when(jnp.logical_not(relayed) & (i >= G * G))
         def _():
-            remote(
-                sbuf.at[s], recv_hbm.at[h, r, c], ssem.at[sent], rsem.at[h * G + c], (th, tr, tc)
-            ).start()
-
-        @pl.when(here)
-        def _():
-            pltpu.make_async_copy(sbuf.at[s], recv_hbm.at[h, r, c], rsem.at[h * G + c]).start()
+            make()
+
+            @pl.when(jnp.logical_not(here))
+            def _():
+                remote(
+                    sbuf.at[s],
+                    recv_hbm.at[h, r, c],
+                    ssem.at[sent],
+                    rsem.at[h * G + c],
+                    (th, tr, tc),
+                ).start()
+
+            @pl.when(here)
+            def _():
+                pltpu.make_async_copy(sbuf.at[s], recv_hbm.at[h, r, c], rsem.at[h * G + c]).start()
 
         return 0
 
-    lax.fori_loop(0, G * G, block, 0)
+    lax.fori_loop(0, 2 * G * G, block, 0)
 
     four = pcol_hbm.at[pl.ds(0, 4)]
     three = pcol_hbm.at[pl.ds(0, 3)]
@@ -381,7 +399,7 @@
             dma((RELAY_SLOTS,)),
         ],
         compiler_params=pltpu.CompilerParams(
-            collective_id=0, has_side_effects=True, vmem_limit_bytes=34 << 20
+            collective_id=0, has_side_effects=True, vmem_limit_bytes=36 << 20
         ),
         name="exchange",
     )(q, block, crow, ccol, prow, pcol, cinv, pinv)

time: 232 us -> 206 us (0.89)
  the two profiles are of different devices: /device:TPU:39 before, /device:TPU:110 now
where the time goes in v3:
time: 206 us
  Pallas kernels  194 us (94%)
  local copies, waits for them, and re-layouts  11.1 us (5%)
    pallas_call x1, Pallas kernels, exchange(): pl.pallas_call(exchange_kernel, out_shape=(pltpu.VMEM((2, G, G, T, T), BF...  179 us
    pallas_call x1, Pallas kernels, assemble(): pl.pallas_call(assemble_kernel, out_shape=jax.ShapeDtypeStruct((2 * G, T,...  15.1 us
    unnamed x8, local copies, waits for them, and re-layouts  5.76 us

profile of v3, /device:TPU:110, one launch (start us, length us, event | category | flops | bytes accessed | tf_op | source)
XLA Modules:
  0.0 206.0 jit_solution(12672762002929258413)
XLA Ops:
  0.0 0.1 sub.37
  0.1 0.8 reshape.68
  0.8 0.1 slice_reduce_fusion
  1.0 0.1 squeeze.9
  1.1 0.2 select_reduce_fusion
  1.3 0.0 copy-start.1
  1.3 0.1 pad_add_fusion.info_ref
  1.4 0.9 copy.36
  2.3 0.6 gather_fusion
  2.9 0.9 copy.35
  3.8 0.6 gather_fusion.1
  4.4 0.8 broadcast_select_fusion
  5.2 1.6 copy.26
  6.7 1.6 copy.34
  8.3 1.6 copy.33
  9.9 1.6 copy.27
  11.5 0.0 copy-done.1
  11.5 178.7 %exchange.1 = (bf16[2,8,8,256,256]{4,3,2,1,0:T(8,128)(2,1)S(1)}, bf16[8,256,256]{2,1,0:T(8,128)(2,1)S(1)}, bf16[16,256,256]{2,1,0:T(8,128)(2,1)S(1)}) custom-call(s32[8]{0:T(128)} %copy-done.1, bf16[8,256,8,256]{3,2,1,0:T(8,128)(2,1)} %bitcast.39, bf16[8,32,256]{2,1,0:T(8,128)(2,1)} %get-tuple-element.17.crow_ref, ...), custom_call_target="tpu_custom_call" | custom-call | tf_op jit(solution)/shard_map/exchange/pallas_call | solution.py:370
  190.1 0.0 copy-start
  190.2 0.7 copy-done
  190.9 15.1 %assemble.1 = bf16[16,256,8,256]{3,2,1,0:T(8,128)(2,1)} custom-call(s32[16]{0:T(128)S(1)} %get-tuple-element.15.rows_ref, s32[16]{0:T(128)S(1)} %get-tuple-element.14.cols_ref, s32[18]{0:T(128)S(1)} %pad_add_fusion.info_ref, bf16[2,8,8,256,256]{4,3,2,1,0:T(8,128)(2,1)S(1)} %get-tuple-element.9.recv_ref, bf16[8,256,256]{2,1,0:T(8,128)(2,1)S(1)} %get-tuple-element.10.v_ref, ...), custom_call_target="tpu_custom_call" | custom-call | tf_op jit(solution)/shard_map/assemble/pallas_call | solution.py:447
  (8 shorter events, 0.1 us)
Async XLA Ops:
  1.3 10.2 %copy-start.1 = (s32[8]{0:T(128)}, s32[8]{0:T(128)S(1)}, u32[]{:S(2)}) copy-start(s32[8]{0:T(128)S(1)} %get-tuple-element.13.q_ref) | copy-start | bytes 100
  190.1 0.7 copy-start

commit v4 on v3

--- a/solution.py
+++ b/solution.py
@@ -51,18 +51,18 @@
 
 
 def turn_of(i):
-    return 3 * i % G, (2 * (i // G) + i // (4 * G) + i) % G
+    return 5 * i % G, (2 * (i // G) + i // (4 * G) + i) % G
 
 
 def exchange_kernel(
     q_ref,
     block_hbm,
-    crow_ref,
-    ccol_ref,
-    prow_ref,
-    pcol_ref,
-    cinv_ref,
-    pinv_ref,
+    crow_in,
+    ccol_in,
+    prow_in,
+    pcol_in,
+    cinv_in,
+    pinv_in,
     recv_hbm,
     v_ref,
     pcol_hbm,
@@ -77,6 +77,13 @@
     lbuf,
     prowg,
     zeros,
+    crow_ref,
+    ccol_ref,
+    prow_ref,
+    pcol_ref,
+    cinv_ref,
+    pinv_ref,
+    natural,
     stage_sem,
     row_sem,
     col_sem,
@@ -123,6 +130,33 @@
         return 0
 
     lax.fori_loop(0, 128, greet, 0)
+
+    def blocks(panel, count, put):
+        deep = panel.shape[0]
+        x = panel[...].astype(F32).reshape(deep * count, T)
+        for lane in range(2):
+            tile[lane, pl.ds(0, deep * count), :] = x[:, lane * L : lane * L + L]
+        for k in range(count):
+            for lane in range(2):
+                put[k, pl.ds(0, deep), pl.ds(lane * L, L)] = tile[
+                    lane, pl.ds(k, deep, stride=count), :
+                ].astype(BF)
+
+    blocks(crow_in, G, natural)
+    for k in range(G):
+        crow_ref[k] = natural[q_ref[k]]
+    blocks(ccol_in, G, natural)
+    for k in range(G):
+        ccol_ref[k] = natural[q_ref[k]]
+    blocks(prow_in, G, prow_ref)
+    blocks(pcol_in, 2 * G, pcol_ref)
+    for x in range(4):
+        for core in range(2):
+            cinv_ref[pl.ds((core * 4 + x) * 32, 32), :] = cinv_in[pl.ds((x * 2 + core) * 32, 32), :]
+            for half in range(2):
+                pinv_ref[pl.ds((core * 8 + half * 4 + x) * 16, 16), :] = pinv_in[
+                    pl.ds((half * 8 + x * 2 + core) * 16, 16), :
+                ]
     pl.semaphore_wait(barrier, 127)
 
     other = (1 - h, r, c)
@@ -166,13 +200,13 @@
         to = (h, r, (c + 2 * t) % G)
         remote(ccol_ref, colg.at[:, ccol_part, :], col_sem.at[0], col_sem.at[2], to).start()
     pltpu.make_async_copy(ccol_ref, colg.at[:, ccol_part, :], col_sem.at[2]).start()
+    rows_on(rowg, row_sem)
     remote(pcol_ref, pcol_hbm.at[:, pcol_part, :], pcol_sem.at[0], pcol_sem.at[3], other).start()
     rows_out(prow_ref, prowg, prow_sem)
     for t in range(1, 4):
         to = (h, r, (c + 2 * t) % G)
         remote(pcol_ref, pcol_hbm.at[:, pcol_part, :], pcol_sem.at[0], pcol_sem.at[4], to).start()
     pltpu.make_async_copy(pcol_ref, pcol_hbm.at[:, pcol_part, :], pcol_sem.at[4]).start()
-    rows_on(rowg, row_sem)
 
     def split(k, _):
         s = k % 2
@@ -204,13 +238,13 @@
     half_part = colg.at[:, ccol_core, :]
     remote(half_part, half_part, col_sem.at[0], col_sem.at[2], twin).wait_recv()
     remote(half_part, half_part, col_sem.at[1], col_sem.at[3], twin).start()
-    rows_on(prowg, prow_sem)
-    part = pcol_hbm.at[:, pcol_over, :]
-    remote(part, part, pcol_sem.at[0], pcol_sem.at[3], other).wait_recv()
-    for t in range(1, 4):
-        to = (h, r, (c + 2 * t) % G)
-        remote(part, part, pcol_sem.at[1], pcol_sem.at[5], to).start()
-
+    remote(half_part, half_part, col_sem.at[1], col_sem.at[3], twin).wait_recv()
+
+    def turn(k, _):
+        colt[k] = colg[k].T
+        return 0
+
+    lax.fori_loop(0, G, turn, 0)
     rows_in(rowg, row_sem)
 
     def scale(k, _):
@@ -218,13 +252,6 @@
         return 0
 
     lax.fori_loop(0, G, scale, 0)
-    remote(half_part, half_part, col_sem.at[1], col_sem.at[3], twin).wait_recv()
-
-    def turn(k, _):
-        colt[k] = colg[k].T
-        return 0
-
-    lax.fori_loop(0, G, turn, 0)
 
     def block(i, _):
         d, dd = turn_of(i % (G * G))
@@ -271,14 +298,15 @@
 
         return 0
 
-    lax.fori_loop(0, 2 * G * G, block, 0)
-
-    four = pcol_hbm.at[pl.ds(0, 4)]
-    three = pcol_hbm.at[pl.ds(0, 3)]
-    remote(four, four, pcol_sem.at[0], pcol_sem.at[4], other).wait_recv()
-    remote(three, three, pcol_sem.at[0], pcol_sem.at[5], other).wait_recv()
-    part = pcol_hbm.at[:, pcol_core, :]
-    remote(part, part, pcol_sem.at[2], pcol_sem.at[6], twin).start()
+    lax.fori_loop(0, G * G, block, 0)
+    rows_on(prowg, prow_sem)
+    part = pcol_hbm.at[:, pcol_over, :]
+    remote(part, part, pcol_sem.at[0], pcol_sem.at[3], other).wait_recv()
+    for t in range(1, 4):
+        to = (h, r, (c + 2 * t) % G)
+        remote(part, part, pcol_sem.at[1], pcol_sem.at[5], to).start()
+
+    lax.fori_loop(G * G, 2 * G * G, block, 0)
 
     for hs in range(2):
         for cs in range(G):
@@ -317,6 +345,13 @@
 
             lax.fori_loop(0, G * G, forward, 0)
 
+    four = pcol_hbm.at[pl.ds(0, 4)]
+    three = pcol_hbm.at[pl.ds(0, 3)]
+    remote(four, four, pcol_sem.at[0], pcol_sem.at[4], other).wait_recv()
+    remote(three, three, pcol_sem.at[0], pcol_sem.at[5], other).wait_recv()
+    part = pcol_hbm.at[:, pcol_core, :]
+    remote(part, part, pcol_sem.at[2], pcol_sem.at[6], twin).start()
+
     rows_in(prowg, prow_sem)
 
     def pscale(k, _):
@@ -388,6 +423,13 @@
             pltpu.VMEM((RELAY_SLOTS * G, T, T), BF),
             pltpu.VMEM((G, T, T), BF),
             pltpu.VMEM((G, T, T), BF),
+            pltpu.VMEM((G, 32, T), BF),
+            pltpu.VMEM((G, 32, T), BF),
+            pltpu.VMEM((G, 32, T), BF),
+            pltpu.VMEM((2 * G, 16, T), BF),
+            pltpu.VMEM((T, T), BF),
+            pltpu.VMEM((T, T), BF),
+            pltpu.VMEM((G, 32, T), BF),
             dma((2,)),
             dma((5,)),
             dma((4,)),
@@ -399,21 +441,29 @@
             dma((RELAY_SLOTS,)),
         ],
         compiler_params=pltpu.CompilerParams(
-            collective_id=0, has_side_effects=True, vmem_limit_bytes=36 << 20
+            collective_id=0, has_side_effects=True, vmem_limit_bytes=37 << 20
         ),
         name="exchange",
     )(q, block, crow, ccol, prow, pcol, cinv, pinv)
 
 
+OUT_SLOTS = 4
+
+
 def assemble_kernel(
-    rows_ref, cols_ref, info_ref, recv_ref, v_ref, pcol_ref, diag_ref, out_ref, tile
+    rows_ref, cols_ref, info_ref, recv_ref, v_ref, pcol_ref, diag_ref, out_hbm, tile, done, sem
 ):
-    k = pl.program_id(0)
-    odd = pl.program_id(1)
+    a = pl.program_id(0)
+    k = a // 2
+    odd = a % 2
+    slot = a % OUT_SLOTS
     live = [info_ref[2 + hs * G + k] == odd for hs in range(2)]
 
+    def put(s, row):
+        return pltpu.make_async_copy(done.at[s], out_hbm.at[row], sem.at[s])
+
     def fill(parts):
-        pc = pcol_ref[0].T
+        pc = pcol_ref[a].T
         for b in range(G):
             acc = jnp.dot(pc, v_ref[b], preferred_element_type=F32)
             for hs in parts:
@@ -430,34 +480,43 @@
     def _():
         i = lax.broadcasted_iota(jnp.int32, (T, T), 0)
         j = lax.broadcasted_iota(jnp.int32, (T, T), 1)
-        extra = jnp.where(i == j, diag_ref[0], 0.0)
+        extra = jnp.where(i == j, diag_ref[a], 0.0)
         for lane in range(2):
             tile[lane, pl.ds(k, T, stride=G), :] += extra[:, lane * L : lane * L + L]
 
+    @pl.when(a >= OUT_SLOTS)
+    def _():
+        put(slot, a).wait()
+
     for m in range(8):
         for lane in range(2):
-            out_ref[0, pl.ds(m * 32, 32), :, pl.ds(lane * L, L)] = (
+            done[slot, pl.ds(m * 32, 32), :, pl.ds(lane * L, L)] = (
                 tile[lane, pl.ds(m * 256, 256), :].reshape(32, G, L).astype(BF)
             )
+    put(slot, a).start()
+
+    @pl.when(a == 2 * G - 1)
+    def _():
+        for s in range(OUT_SLOTS):
+            put(s, a).wait()
 
 
 def assemble(rows, cols, info, recv, v, pcol, diag):
-    whole = pl.BlockSpec((G, T, T), lambda k, o, *_: (0, 0, 0))
     recv, v, pcol = (pltpu.with_memory_space_constraint(x, pltpu.VMEM) for x in (recv, v, pcol))
+    vmem = pl.BlockSpec(memory_space=pltpu.VMEM)
     return pl.pallas_call(
         assemble_kernel,
         out_shape=jax.ShapeDtypeStruct((2 * G, T, G, T), BF),
         grid_spec=pltpu.PrefetchScalarGridSpec(
             num_scalar_prefetch=3,
-            grid=(G, 2),
-            in_specs=[
-                pl.BlockSpec(memory_space=pltpu.VMEM),
-                whole,
-                pl.BlockSpec((1, T, T), lambda k, o, *_: (2 * k + o, 0, 0)),
-                pl.BlockSpec((1, 1, T), lambda k, o, *_: (2 * k + o, 0, 0)),
+            grid=(2 * G,),
+            in_specs=[vmem] * 4,
+            out_specs=pl.BlockSpec(memory_space=pl.ANY),
+            scratch_shapes=[
+                pltpu.VMEM((2, T * G, L), F32),
+                pltpu.VMEM((OUT_SLOTS, T, G, T), BF),
+                pltpu.SemaphoreType.DMA((OUT_SLOTS,)),
             ],
-            out_specs=pl.BlockSpec((1, T, G, T), lambda k, o, *_: (2 * k + o, 0, 0, 0)),
-            scratch_shapes=[pltpu.VMEM((2, T * G, L), F32)],
         ),
         compiler_params=pltpu.CompilerParams(vmem_limit_bytes=12 << 20),
         name="assemble",
@@ -485,18 +544,15 @@
     ).astype(jnp.int32)
     q = lax.dynamic_index_in_dim(source, h, 0, keepdims=False)
 
-    def ordered(x):
-        x = x.reshape(x.shape[1], G, T)
-        return jnp.swapaxes(jnp.take(x, q, axis=1), 0, 1)
-
-    crow = ordered(child_row)
-    ccol = ordered(child_col)
-    prow = jnp.swapaxes(parent_row.reshape(-1, G, T), 0, 1)
-    pcol = jnp.swapaxes(parent_col.reshape(-1, 2 * G, T), 0, 1)
-    cinv = jnp.swapaxes(child_pivot_inv.reshape(4, 2, 32, T), 0, 1).reshape(T, T)
-    pinv = jnp.transpose(parent_pivot_inv.reshape(2, 4, 2, 16, T), (2, 0, 1, 3, 4)).reshape(T, T)
     recv, v, pcols = exchange(
-        q, child_block.reshape(G, T, G, T), crow, ccol, prow, pcol, cinv, pinv
+        q,
+        child_block.reshape(G, T, G, T),
+        child_row.reshape(-1, G, T),
+        child_col.reshape(-1, G, T),
+        parent_row.reshape(-1, G, T),
+        parent_col.reshape(-1, 2 * G, T),
+        child_pivot_inv[0],
+        parent_pivot_inv,
     )
     rows = ((r - shift) % G).reshape(-1)
     cols = ((c - shift) % G).reshape(-1)

time: 206 us -> 188 us (0.913)
  the two profiles are of different devices: /device:TPU:110 before, /device:TPU:15 now
where the time goes in v4:
time: 188 us; the launch traced here: 186 us
  Pallas kernels  183 us (97%)
  local copies, waits for them, and re-layouts  2.31 us (1%)
    pallas_call x1, Pallas kernels, exchange(): pl.pallas_call(exchange_kernel, out_shape=(pltpu.VMEM((2, G, G, T, T), BF...  170 us
    pallas_call x1, Pallas kernels, assemble(): pl.pallas_call(assemble_kernel, out_shape=jax.ShapeDtypeStruct((2 * G, T,...  13.8 us

profile of v4, /device:TPU:15, one launch (start us, length us, event | category | flops | bytes accessed | tf_op | source)
XLA Modules:
  0.0 186.0 jit_solution(11096513621913834691)
XLA Ops:
  0.0 0.1 sub.37
  0.1 0.8 reshape.51
  0.8 0.1 slice_reduce_fusion
  1.0 0.1 squeeze.12
  1.1 0.2 select_reduce_fusion
  1.2 0.5 dynamic-slice_bitcast_fusion.q_ref
  1.8 0.1 pad_add_fusion.info_ref
  1.9 169.6 %exchange.1 = (bf16[2,8,8,256,256]{4,3,2,1,0:T(8,128)(2,1)S(1)}, bf16[8,256,256]{2,1,0:T(8,128)(2,1)S(1)}, bf16[16,256,256]{2,1,0:T(8,128)(2,1)S(1)}) custom-call(s32[8]{0:T(128)} %dynamic-slice_bitcast_fusion.q_ref, bf16[8,256,8,256]{3,2,1,0:T(8,128)(2,1)} %bitcast.13, bf16[32,8,256]{2,1,0:T(8,128)(2,1)} %bitcast.14, bf16[32,8,256]{2,1,0:T(8,128)(2,1)} %bitcast.15, ...), custom_call_target="tpu_custom_call" | custom-call | tf_op jit(solution)/shard_map/exchange/pallas_call | solution.py:405
  171.4 0.0 copy-start
  171.4 0.7 copy-done
  172.2 13.8 %assemble.1 = bf16[16,256,8,256]{3,2,1,0:T(8,128)(2,1)} custom-call(s32[16]{0:T(128)S(1)} %get-tuple-element.12.rows_ref, s32[16]{0:T(128)S(1)} %get-tuple-element.11.cols_ref, s32[18]{0:T(128)S(1)} %pad_add_fusion.info_ref, bf16[2,8,8,256,256]{4,3,2,1,0:T(8,128)(2,1)S(1)} %get-tuple-element.8.recv_ref, bf16[8,256,256]{2,1,0:T(8,128)(2,1)S(1)} %get-tuple-element.9.v_ref, ...), custom_call_target="tpu_custom_call" | custom-call | tf_op jit(solution)/shard_map/assemble/pallas_call | solution.py:507
  (5 shorter events, 0.0 us)
Async XLA Ops:
  171.4 0.7 copy-start

commit v5 on v4

--- a/solution.py
+++ b/solution.py
@@ -55,7 +55,7 @@
 
 
 def exchange_kernel(
-    q_ref,
+    map_ref,
     block_hbm,
     crow_in,
     ccol_in,
@@ -84,6 +84,7 @@
     cinv_ref,
     pinv_ref,
     natural,
+    q_ref,
     stage_sem,
     row_sem,
     col_sem,
@@ -130,6 +131,13 @@
         return 0
 
     lax.fori_loop(0, 128, greet, 0)
+
+    moves = [map_ref[h, G * k] - 2 * G * k for k in range(G)]
+    for d in range(G):
+        found = jnp.int32(0)
+        for k in range(G):
+            found = found + jnp.where(moves[k] == d, k, 0)
+        q_ref[d] = found
 
     def blocks(panel, count, put):
         deep = panel.shape[0]
@@ -397,7 +405,7 @@
             remote(sbuf.at[pl.ds(0, G)], dst, ssem.at[0], rsem.at[hs * G + cs], other).wait_recv()
 
 
-def exchange(q, block, crow, ccol, prow, pcol, cinv, pinv):
+def exchange(child_map, block, crow, ccol, prow, pcol, cinv, pinv):
     any_space = pl.BlockSpec(memory_space=pl.ANY)
     vmem = pl.BlockSpec(memory_space=pltpu.VMEM)
     smem = pl.BlockSpec(memory_space=pltpu.SMEM)
@@ -430,6 +438,7 @@
             pltpu.VMEM((T, T), BF),
             pltpu.VMEM((T, T), BF),
             pltpu.VMEM((G, 32, T), BF),
+            pltpu.SMEM((G,), jnp.int32),
             dma((2,)),
             dma((5,)),
             dma((4,)),
@@ -444,20 +453,30 @@
             collective_id=0, has_side_effects=True, vmem_limit_bytes=37 << 20
         ),
         name="exchange",
-    )(q, block, crow, ccol, prow, pcol, cinv, pinv)
+    )(child_map, block, crow, ccol, prow, pcol, cinv, pinv)
 
 
 OUT_SLOTS = 4
 
 
 def assemble_kernel(
-    rows_ref, cols_ref, info_ref, recv_ref, v_ref, pcol_ref, diag_ref, out_hbm, tile, done, sem
+    map_ref, recv_ref, v_ref, pcol_ref, diag_hbm, out_hbm, tile, done, diag_ref, sem, diag_sem
 ):
+    h = lax.axis_index("half")
+    r = lax.axis_index("row")
+    c = lax.axis_index("col")
     a = pl.program_id(0)
     k = a // 2
     odd = a % 2
     slot = a % OUT_SLOTS
-    live = [info_ref[2 + hs * G + k] == odd for hs in range(2)]
+    fetch = pltpu.make_async_copy(diag_hbm, diag_ref, diag_sem)
+    pl.when((r == c) & (a == 0))(fetch.start)
+    moved = [map_ref[hs, G * k] - 2 * G * k for hs in range(2)]
+    live = [(moved[hs] > r).astype(jnp.int32) == odd for hs in range(2)]
+
+    def came(hs, b):
+        col = (c - (map_ref[hs, G * b] - 2 * G * b) + G) % G
+        return recv_ref[hs, (r - moved[hs] + G) % G, col].astype(F32)
 
     def put(s, row):
         return pltpu.make_async_copy(done.at[s], out_hbm.at[row], sem.at[s])
@@ -467,7 +486,7 @@
         for b in range(G):
             acc = jnp.dot(pc, v_ref[b], preferred_element_type=F32)
             for hs in parts:
-                acc = acc + recv_ref[hs, rows_ref[hs * G + k], cols_ref[hs * G + b]].astype(F32)
+                acc = acc + came(hs, b)
             for lane in range(2):
                 tile[lane, pl.ds(b, T, stride=G), :] = acc[:, lane * L : lane * L + L]
 
@@ -476,8 +495,9 @@
     pl.when(live[1] & jnp.logical_not(live[0]))(lambda: fill((1,)))
     pl.when(jnp.logical_not(live[0] | live[1]))(lambda: fill(()))
 
-    @pl.when((info_ref[0] == 1) & (info_ref[1] == odd))
+    @pl.when((r == c) & (h == odd))
     def _():
+        pl.when(k == 0)(fetch.wait)
         i = lax.broadcasted_iota(jnp.int32, (T, T), 0)
         j = lax.broadcasted_iota(jnp.int32, (T, T), 1)
         extra = jnp.where(i == j, diag_ref[a], 0.0)
@@ -501,26 +521,31 @@
             put(s, a).wait()
 
 
-def assemble(rows, cols, info, recv, v, pcol, diag):
+def assemble(child_map, recv, v, pcol, diag):
     recv, v, pcol = (pltpu.with_memory_space_constraint(x, pltpu.VMEM) for x in (recv, v, pcol))
+    child_map, diag = (
+        pltpu.with_memory_space_constraint(x, pltpu.HBM) for x in (child_map, diag)
+    )
     vmem = pl.BlockSpec(memory_space=pltpu.VMEM)
     return pl.pallas_call(
         assemble_kernel,
         out_shape=jax.ShapeDtypeStruct((2 * G, T, G, T), BF),
         grid_spec=pltpu.PrefetchScalarGridSpec(
-            num_scalar_prefetch=3,
+            num_scalar_prefetch=1,
             grid=(2 * G,),
-            in_specs=[vmem] * 4,
+            in_specs=[vmem] * 3 + [pl.BlockSpec(memory_space=pl.ANY)],
             out_specs=pl.BlockSpec(memory_space=pl.ANY),
             scratch_shapes=[
                 pltpu.VMEM((2, T * G, L), F32),
                 pltpu.VMEM((OUT_SLOTS, T, G, T), BF),
+                pltpu.VMEM((2 * G, 1, T), F32),
                 pltpu.SemaphoreType.DMA((OUT_SLOTS,)),
+                pltpu.SemaphoreType.DMA,
             ],
         ),
         compiler_params=pltpu.CompilerParams(vmem_limit_bytes=12 << 20),
         name="assemble",
-    )(rows, cols, info, recv, v, pcol, diag)
+    )(child_map, recv, v, pcol, diag)
 
 
 def shards(
@@ -534,18 +559,8 @@
     parent_pivot_inv,
     parent_diag,
 ):
-    h = lax.axis_index("half")
-    r = lax.axis_index("row")
-    c = lax.axis_index("col")
-    steps = jnp.arange(G, dtype=jnp.int32)
-    shift = child_map.reshape(2, G, G)[:, :, 0] - 2 * G * steps[None, :]
-    source = jnp.sum(
-        jnp.where(shift[:, None, :] == steps[None, :, None], steps[None, None, :], 0), axis=2
-    ).astype(jnp.int32)
-    q = lax.dynamic_index_in_dim(source, h, 0, keepdims=False)
-
     recv, v, pcols = exchange(
-        q,
+        child_map,
         child_block.reshape(G, T, G, T),
         child_row.reshape(-1, G, T),
         child_col.reshape(-1, G, T),
@@ -554,12 +569,7 @@
         child_pivot_inv[0],
         parent_pivot_inv,
     )
-    rows = ((r - shift) % G).reshape(-1)
-    cols = ((c - shift) % G).reshape(-1)
-    carry = (shift > r).astype(jnp.int32).reshape(-1)
-    head = jnp.stack([(r == c).astype(jnp.int32), h.astype(jnp.int32)])
-    info = jnp.concatenate([head, carry])
-    out = assemble(rows, cols, info, recv, v, pcols, parent_diag)
+    out = assemble(child_map, recv, v, pcols, parent_diag)
     return out.reshape(2 * G, 1, T, G, 1, T)
 
 

time: 188 us -> 185 us (0.984)
  local copies, waits for them, and re-layouts: 2.31 us -> 0 us
where the time goes in v5:
time: 185 us; the launch traced here: 184 us
  Pallas kernels  184 us (99%)
    pallas_call x1, Pallas kernels, exchange(): pl.pallas_call(exchange_kernel, out_shape=(pltpu.VMEM((2, G, G, T, T), BF...  170 us
    pallas_call x1, Pallas kernels, assemble(): pl.pallas_call(assemble_kernel, out_shape=jax.ShapeDtypeStruct((2 * G, T,...  14.3 us

profile of v5, /device:TPU:15, one launch (start us, length us, event | category | flops | bytes accessed | tf_op | source)
XLA Modules:
  0.0 184.1 jit_solution(1105868186017786029)
XLA Ops:
  0.0 169.8 %exchange.1 = (bf16[2,8,8,256,256]{4,3,2,1,0:T(8,128)(2,1)S(1)}, bf16[8,256,256]{2,1,0:T(8,128)(2,1)S(1)}, bf16[16,256,256]{2,1,0:T(8,128)(2,1)S(1)}) custom-call(s32[2,64]{1,0:T(2,128)} %map_ref.3, bf16[8,256,8,256]{3,2,1,0:T(8,128)(2,1)} %bitcast.9, bf16[32,8,256]{2,1,0:T(8,128)(2,1)} %bitcast.10, bf16[32,8,256]{2,1,0:T(8,128)(2,1)} %bitcast.11, ...), custom_call_target="tpu_custom_call" | custom-call | tf_op jit(solution)/shard_map/exchange/pallas_call | solution.py:413
  169.8 14.3 %assemble.1 = bf16[16,256,8,256]{3,2,1,0:T(8,128)(2,1)} custom-call(s32[2,64]{1,0:T(2,128)} %map_ref.3, bf16[2,8,8,256,256]{4,3,2,1,0:T(8,128)(2,1)S(1)} %get-tuple-element.8.recv_ref, bf16[8,256,256]{2,1,0:T(8,128)(2,1)S(1)} %get-tuple-element.9.v_ref, bf16[16,256,256]{2,1,0:T(8,128)(2,1)S(1)} %get-tuple-element.10.pcol_ref, f32[16,1,256]{2,1,0:T(1,128)} %diag_hbm.1), custom_call_target="tpu_custom_call" | custom-call | tf_op jit(solution)/shard_map/assemble/pallas_call | solution.py:530
